TPU v7x, 32 devices: a whole 2x2x4 slice. The times are simulated.
32 devices in a mesh: gx: 4 (over y, x), gy: 2 (over core), gz: 4 (over z).
Axes of the slice: x: 2, y: 2, z: 4, core: 2. Of those that a mesh axis runs over, the one named last changes fastest.
Arguments:
- positions: float32 [3, 4, 4, 8, 128], P(None, 'gx', 'gy', 'gz'), may hold values from 0 to 1
- velocities: float32 [3, 4, 4, 8, 128], P(None, 'gx', 'gy', 'gz'), may hold values from -1.8 to 1.8
- species: int32 [4, 4, 8, 128], P('gx', 'gy', 'gz'), may hold values from 0 to 1
- counts: int32 [4, 4, 8], P('gx', 'gy', 'gz'), may hold values from 32 to 128
Outputs:
- new_positions: float32 [3, 4, 4, 8, 128], P(None, 'gx', 'gy', 'gz')
- new_velocities: float32 [3, 4, 4, 8, 128], P(None, 'gx', 'gy', 'gz')
All inputs are finite; a program needn't handle non-finite values.
Results may differ from a plain program's by a relative error of at most 0.0003.
Values sent between devices are 32-bit elements; how exact they have to be, the bound alone decides.
No kernel may reach another device: no remote copies, remote signals or barrier semaphores. Data moves between devices by JAX's collectives and lax.ppermute only.
A program may use at most 64 MiB of HBM per device.

v0:
```python
import functools

import jax
import jax.numpy as jnp
from jax import lax
from jax.experimental import pallas as pl
from jax.experimental.pallas import tpu as pltpu
from jax.sharding import PartitionSpec as P

time_step = 0.05
half_kick = 0.5 * time_step
LANES = 128
ROOT = 1.3 ** (1.0 / 3.0)


def ring_halo(cells, axis, dim, width):
    count = lax.axis_size(axis)
    size = cells.shape[dim]
    head = lax.slice_in_dim(cells, 0, width, axis=dim)
    tail = lax.slice_in_dim(cells, size - width, size, axis=dim)
    if count == 1:
        return jnp.concatenate([tail, cells, head], axis=dim)
    if count == 2 and size == 2 * width:
        other = lax.ppermute(cells, axis, [(0, 1), (1, 0)])
        return jnp.concatenate(
            [
                lax.slice_in_dim(other, width, size, axis=dim),
                cells,
                lax.slice_in_dim(other, 0, width, axis=dim),
            ],
            axis=dim,
        )
    below = lax.ppermute(tail, axis, [(i, (i + 1) % count) for i in range(count)])
    above = lax.ppermute(head, axis, [((i + 1) % count, i) for i in range(count)])
    return jnp.concatenate([below, cells, above], axis=dim)


def by_code(code, first, second):
    return jnp.where(code > 1.5, second, jnp.where(code > 0.5, first, 0.0))


def split3(value):
    high = value.astype(jnp.bfloat16).astype(jnp.float32)
    rest = value - high
    middle = rest.astype(jnp.bfloat16).astype(jnp.float32)
    return high, middle, rest - middle


def row_masks():
    row = lax.broadcasted_iota(jnp.int32, (8, LANES), 0)
    masks = [(row == k).astype(jnp.float32) for k in range(5)]
    return masks, masks[0] + masks[1] + masks[2]


def placed(tile, centre, masks, spatial):
    point = tile * spatial
    for axis in range(3):
        if centre[axis]:
            point = point + centre[axis] * masks[axis]
    return point, jnp.sum(point * point, axis=0, keepdims=True)


def partner_features(tile, centre, masks, spatial):
    point, norm = placed(tile, centre, masks, spatial)
    scale = by_code(tile[3:4], 1.0, ROOT)
    row = (point - norm * masks[3] + masks[4]) * scale
    high, middle, low = split3(row)
    first = jnp.concatenate([high, middle], axis=0).astype(jnp.bfloat16)
    last = jnp.concatenate([low, high], axis=0).astype(jnp.bfloat16)
    return point, jnp.concatenate([first, first, last], axis=0)


def target_features(tile, centre, masks, spatial):
    point, norm = placed(tile, centre, masks, spatial)
    high, middle, low = split3(2.0 * point + masks[3] + (1.0 - norm) * masks[4])
    stacked = jnp.concatenate([high, high, middle, middle, high, low], axis=0)
    return point, jnp.transpose(stacked).astype(jnp.bfloat16)


def centre_of(cell, extent):
    return tuple(float(c) - 0.5 * e for c, e in zip(cell, extent))


def density_kernel(extent, feat_ref, slope_ref, part_ref):
    ex, ey, ez = extent
    masks, spatial = row_masks()
    for a in range(ex):
        for b in range(ey):
            for c in range(ez):
                index = (a * ey + b) * ez + c
                _, block = partner_features(
                    feat_ref[index], centre_of((a, b, c), extent), masks, spatial
                )
                part_ref[:, index * LANES : (index + 1) * LANES] = block
    place = 0
    rows = 64
    for a in range(1, ex - 1):
        for b in range(1, ey - 1):
            for c in range(1, ez - 1):
                index = (a * ey + b) * ez + c
                tile = feat_ref[index]
                _, left = target_features(tile, centre_of((a, b, c), extent), masks, spatial)
                sums = []
                for start in range(0, LANES, rows):
                    total = jnp.zeros((rows, LANES), jnp.float32)
                    for p in (-1, 0, 1):
                        for q in (-1, 0, 1):
                            base = ((a + p) * ey + b + q) * ez + c - 1
                            near = jnp.dot(
                                left[start : start + rows],
                                part_ref[:, base * LANES : (base + 3) * LANES],
                                preferred_element_type=jnp.float32,
                            )
                            for k in range(3):
                                part = jnp.maximum(near[:, k * LANES : (k + 1) * LANES], 0.0)
                                if p == 0 and q == 0 and k == 1:
                                    i = lax.broadcasted_iota(jnp.int32, (rows, LANES), 0)
                                    j = lax.broadcasted_iota(jnp.int32, (rows, LANES), 1)
                                    part = jnp.where(i + start == j, 0.0, part)
                                total = total + part * part * part
                    sums.append(total)
                density = jnp.sum(jnp.transpose(jnp.concatenate(sums, axis=0)), axis=0, keepdims=True)
                present = by_code(tile[3:4], 1.0, 1.0)
                slope_ref[place : place + 1, :] = -0.5 * present / jnp.sqrt(density + 1.0)
                place += 1


def force_kernel(extent, stage, feat_ref, slope_ref, vel_ref, *refs):
    if stage == "last":
        new_vel_ref, part_ref, value_ref = refs
    else:
        new_vel_ref, new_loc_ref, part_ref, value_ref = refs
    ex, ey, ez = extent
    near_z = ez - 2
    masks, spatial = row_masks()
    for a in range(ex):
        for b in range(ey):
            for c in range(near_z):
                index = (a * ey + b) * near_z + c
                tile = feat_ref[(a * ey + b) * ez + c + 1]
                point, block = partner_features(
                    tile, centre_of((a, b, c + 1), extent), masks, spatial
                )
                lanes = slice(index * LANES, (index + 1) * LANES)
                part_ref[:, lanes] = block
                code = tile[3:4]
                slope = slope_ref[index : index + 1, :]
                value_ref[:, lanes] = (
                    point
                    + by_code(code, 3.0, 3.0 * ROOT) * masks[3]
                    + (slope * by_code(code, 3.0, 3.0 / (ROOT * ROOT))) * masks[4]
                )
                value_ref[5:6, lanes] = by_code(code, 0.6, 0.8 / ROOT)
    place = 0
    rows = 32
    for a in range(1, ex - 1):
        for b in range(1, ey - 1):
            for c in range(2, ez - 2):
                tile = feat_ref[(a * ey + b) * ez + c]
                point, left = target_features(tile, centre_of((a, b, c), extent), masks, spatial)
                code = tile[3:4]
                index = (a * ey + b) * near_z + c - 1
                slope = slope_ref[index : index + 1, :]
                solute = code > 1.5
                u = slope * jnp.where(solute, 1.0 / 1.3, 1.0)
                rho = jnp.where(solute, 0.4 / 1.3, 0.3)
                columns = jnp.transpose(u * masks[0] + rho * masks[1])
                sums = [[] for _ in range(4)]
                for start in range(0, LANES, rows):
                    u_i = jnp.broadcast_to(columns[start : start + rows, 0:1], (rows, LANES))
                    rho_i = jnp.broadcast_to(columns[start : start + rows, 1:2], (rows, LANES))
                    total = [jnp.zeros((rows, LANES), jnp.float32) for _ in range(4)]
                    for p in (-1, 0, 1):
                        for q in (-1, 0, 1):
                            base = ((a + p) * ey + b + q) * near_z + c - 2
                            near = jnp.dot(
                                left[start : start + rows],
                                part_ref[:, base * LANES : (base + 3) * LANES],
                                preferred_element_type=jnp.float32,
                            )
                            for k in range(3):
                                lanes = slice((base + k) * LANES, (base + k + 1) * LANES)
                                s = jnp.maximum(near[:, k * LANES : (k + 1) * LANES], 0.0)
                                w = u_i * value_ref[3:4, lanes] + value_ref[4:5, lanes]
                                w = (w * s + rho_i * value_ref[5:6, lanes]) * s
                                total[3] = total[3] + w
                                for axis in range(3):
                                    total[axis] = total[axis] + w * value_ref[axis : axis + 1, lanes]
                    for k in range(4):
                        sums[k].append(total[k])
                flat = [
                    jnp.sum(jnp.transpose(jnp.concatenate(parts, axis=0)), axis=0, keepdims=True)
                    for parts in sums
                ]
                amplitude = by_code(code, 1.0, 1.3)
                kick = half_kick * jnp.where(solute, 1.6, 1.0)
                for axis in range(3):
                    force = -2.0 * amplitude * (flat[axis] - point[axis : axis + 1] * flat[3])
                    speed = vel_ref[place, axis : axis + 1, :] + kick * force
                    if stage == "middle":
                        speed = speed + kick * force
                    new_vel_ref[place, axis : axis + 1, :] = speed
                    if stage != "last":
                        new_loc_ref[place, axis : axis + 1, :] = (
                            tile[axis : axis + 1] + time_step * speed
                        )
                if stage != "last":
                    new_loc_ref[place, 3:4, :] = code
                place += 1


def on_device(positions, velocities, species, counts):
    cx, cy, cz, slots = positions.shape[1:]
    present = lax.broadcasted_iota(jnp.int32, species.shape, 3) < counts[..., None]
    code = jnp.where(present, jnp.where(species == 1, 2.0, 1.0), 0.0)
    location = jnp.concatenate([jnp.moveaxis(positions, 0, 3), code[..., None, :]], axis=3)
    velocity = jnp.moveaxis(velocities, 0, 3).reshape(cx * cy * cz, 3, slots)
    extent = (cx + 2, cy + 2, cz + 4)
    own = cx * cy * cz
    cells = extent[0] * extent[1] * extent[2]
    near = extent[0] * extent[1] * (cz + 2)
    vmem = pl.BlockSpec(memory_space=pltpu.VMEM)

    def evaluate(location, velocity, stage):
        wide = ring_halo(location, "gy", 1, 1)
        wide = ring_halo(wide, "gx", 0, 1)
        wide = ring_halo(wide, "gz", 2, 2)
        feat = jnp.pad(wide.reshape(cells, 4, slots), ((0, 0), (0, 4), (0, 0)))
        slopes = pl.pallas_call(
            functools.partial(density_kernel, extent),
            out_shape=jax.ShapeDtypeStruct((cx * cy * (cz + 2), slots), jnp.float32),
            in_specs=[vmem],
            out_specs=vmem,
            scratch_shapes=[pltpu.VMEM((48, cells * slots), jnp.bfloat16)],
            name="density",
        )(feat)
        slopes = slopes.reshape(cx, cy, cz + 2, slots)
        slopes = ring_halo(slopes, "gy", 1, 1)
        slopes = ring_halo(slopes, "gx", 0, 1).reshape(near, slots)
        out_shape = [jax.ShapeDtypeStruct((own, 3, slots), jnp.float32)]
        if stage != "last":
            out_shape.append(jax.ShapeDtypeStruct((own, 4, slots), jnp.float32))
        out = pl.pallas_call(
            functools.partial(force_kernel, extent, stage),
            out_shape=out_shape,
            in_specs=[vmem] * 3,
            out_specs=[vmem] * len(out_shape),
            scratch_shapes=[
                pltpu.VMEM((48, near * slots), jnp.bfloat16),
                pltpu.VMEM((8, near * slots), jnp.float32),
            ],
            name="force_" + stage,
        )(feat, slopes, velocity)
        if stage == "last":
            return location, out[0]
        return out[1].reshape(location.shape), out[0]

    location, velocity = evaluate(location, velocity, "first")
    location, velocity = evaluate(location, velocity, "middle")
    location, velocity = evaluate(location, velocity, "last")
    new_positions = jnp.moveaxis(location[..., :3, :], 3, 0)
    new_velocities = jnp.moveaxis(velocity.reshape(cx, cy, cz, 3, slots), 3, 0)
    return new_positions, new_velocities


def solution(mesh):
    return jax.shard_map(
        on_device,
        mesh=mesh,
        in_specs=(
            P(None, "gx", "gy", "gz", None),
            P(None, "gx", "gy", "gz", None),
            P("gx", "gy", "gz", None),
            P("gx", "gy", "gz"),
        ),
        out_specs=(P(None, "gx", "gy", "gz", None), P(None, "gx", "gy", "gz", None)),
        check_vma=False,
    )
```

profile of v0, /device:TPU:0, one launch (start us, length us, event | category | flops | bytes accessed | tf_op | source)
XLA Modules:
  0.0 103.0 jit_solution(16536951643889155222)
XLA Ops:
  0.6 0.7 copy-done.7
  1.3 0.8 fusion
  2.1 0.6 collective-permute-start
  2.6 0.8 collective-permute-done
  3.5 3.8 %collective-permute-start.2 = (f32[1,4,2,4,128]{4,2,1,0,3:T(2,128)S(1)}, f32[1,4,2,4,128]{4,2,1,0,3:T(2,128)S(1)}, u32[]{:S(2)}, u32[]{:S(2)}) collective-permute-start(f32[1,4,2,4,128]{4,2,1,0,3:T(2,128)S(1)} %pad_maximum_fusion.9), channel_id=1, source_target_pairs={{8,0},{16,8},{24,16},{0,24},{9,1},{17,9},{25,17},{1,25},{10,2},{18... | collective-permute-start | bytes 49160 | tf_op jit(solution)/shard_map/ppermute | solution.py:34
  7.3 0.0 collective-permute-start.1
  7.3 1.4 %collective-permute-done.2 = f32[1,4,2,4,128]{4,2,1,0,3:T(2,128)S(1)} collective-permute-done((f32[1,4,2,4,128]{4,2,1,0,3:T(2,128)S(1)}, f32[1,4,2,4,128]{4,2,1,0,3:T(2,128)S(1)}, u32[]{:S(2)}, u32[]{:S(2)}) %collective-permute-start.2) | collective-permute-done | bytes 16416 | tf_op jit(solution)/shard_map/ppermute | solution.py:34
  8.7 3.2 %collective-permute-done.1 = f32[1,4,2,4,128]{4,2,1,0,3:T(2,128)S(1)} collective-permute-done((f32[1,4,2,4,128]{4,2,1,0,3:T(2,128)S(1)}, f32[1,4,2,4,128]{4,2,1,0,3:T(2,128)S(1)}, u32[]{:S(2)}, u32[]{:S(2)}) %collective-permute-start.1) | collective-permute-done | bytes 16416 | tf_op jit(solution)/shard_map/ppermute | solution.py:33
  12.0 3.7 %collective-permute-start.4 = (f32[3,4,2,4,128]{4,2,1,0,3:T(2,128)S(1)}, f32[3,4,2,4,128]{4,2,1,0,3:T(2,128)S(1)}, u32[]{:S(2)}, u32[]{:S(2)}) collective-permute-start(f32[3,4,2,4,128]{4,2,1,0,3:T(2,128)S(1)} %pad_maximum_fusion.3), channel_id=1, source_target_pairs={{1,0},{2,1},{3,2},{0,3},{5,4},{6,5},{7,6},{4,7},{9,8},{10,9},{11,1... | collective-permute-start | bytes 147464 | tf_op jit(solution)/shard_map/ppermute | solution.py:34
  15.6 0.0 collective-permute-start.3
  15.6 1.7 %collective-permute-done.4 = f32[3,4,2,4,128]{4,2,1,0,3:T(2,128)S(1)} collective-permute-done((f32[3,4,2,4,128]{4,2,1,0,3:T(2,128)S(1)}, f32[3,4,2,4,128]{4,2,1,0,3:T(2,128)S(1)}, u32[]{:S(2)}, u32[]{:S(2)}) %collective-permute-start.4) | collective-permute-done | bytes 49184 | tf_op jit(solution)/shard_map/ppermute | solution.py:34
  17.4 4.1 %collective-permute-done.3 = f32[3,4,2,4,128]{4,2,1,0,3:T(2,128)S(1)} collective-permute-done((f32[3,4,2,4,128]{4,2,1,0,3:T(2,128)S(1)}, f32[3,4,2,4,128]{4,2,1,0,3:T(2,128)S(1)}, u32[]{:S(2)}, u32[]{:S(2)}) %collective-permute-start.3) | collective-permute-done | bytes 49184 | tf_op jit(solution)/shard_map/ppermute | solution.py:33
  21.5 0.1 pad_maximum_fusion
  21.6 0.1 copy.7
  21.7 0.7 pad.10.feat_ref
  22.4 4.4 %density.3 = f32[8,128]{1,0:T(8,128)} custom-call(f32[72,8,128]{2,1,0:T(8,128)} %pad.10.feat_ref), custom_call_target="tpu_custom_call" | custom-call | tf_op jit(solution)/shard_map/density/pallas_call | solution.py:229
  26.8 0.0 collective-permute-start.5
  26.8 1.4 %collective-permute-done.5 = f32[1,2,4,128]{3,2,1,0:T(4,128)S(1)} collective-permute-done((f32[1,2,4,128]{3,2,1,0:T(4,128)}, f32[1,2,4,128]{3,2,1,0:T(4,128)S(1)}, u32[]{:S(2)}, u32[]{:S(2)}) %collective-permute-start.5) | collective-permute-done | bytes 4128 | tf_op jit(solution)/shard_map/ppermute | solution.py:24
  28.2 0.1 collective-permute-start.7
  28.3 2.0 %collective-permute-start.6 = (f32[1,4,4,128]{3,2,1,0:T(4,128)S(1)}, f32[1,4,4,128]{3,2,1,0:T(4,128)S(1)}, u32[]{:S(2)}, u32[]{:S(2)}) collective-permute-start(f32[1,4,4,128]{3,2,1,0:T(4,128)S(1)} %pad_maximum_fusion.13), channel_id=1, source_target_pairs={{0,8},{8,16},{16,24},{24,0},{1,9},{9,17},{17,25},{25,1},{2,10},{10... | collective-permute-start | bytes 24584 | tf_op jit(solution)/shard_map/ppermute | solution.py:33
  30.3 0.6 copy.8
  30.9 1.0 collective-permute-done.7
  31.9 1.0 collective-permute-done.6
  32.9 0.6 pad_maximum_fusion.6
  33.5 5.7 %force_first.1 = (f32[4,3,128]{2,1,0:T(4,128)}, f32[4,4,128]{2,1,0:T(4,128)}) custom-call(f32[72,8,128]{2,1,0:T(8,128)} %pad.10.feat_ref, f32[48,128]{1,0:T(8,128)} %bitcast.36, f32[4,3,128]{2,1,0:T(4,128)} %bitcast.55), custom_call_target="tpu_custom_call" | custom-call | tf_op jit(solution)/shard_map/force_first/pallas_call | solution.py:243
  39.2 1.4 %collective-permute-done.8 = f32[1,2,2,4,128]{4,3,2,1,0:T(4,128)S(1)} collective-permute-done((f32[1,2,2,4,128]{4,3,2,1,0:T(4,128)}, f32[1,2,2,4,128]{4,3,2,1,0:T(4,128)S(1)}, u32[]{:S(2)}, u32[]{:S(2)}) %collective-permute-start.8) | collective-permute-done | bytes 8224 | tf_op jit(solution)/shard_map/ppermute | solution.py:24
  40.6 1.1 %collective-permute-start.10 = (f32[1,4,2,4,128]{4,3,2,1,0:T(4,128)S(1)}, f32[1,4,2,4,128]{4,3,2,1,0:T(4,128)S(1)}, u32[]{:S(2)}, u32[]{:S(2)}) collective-permute-start(f32[1,4,2,4,128]{4,3,2,1,0:T(4,128)S(1)} %pad_maximum_fusion.10), channel_id=1, source_target_pairs={{8,0},{16,8},{24,16},{0,24},{9,1},{17,9},{25,17},{1,25},{10,2},{18... | collective-permute-start | bytes 49160 | tf_op jit(solution)/shard_map/ppermute | solution.py:34
  41.7 1.0 collective-permute-start.9
  42.6 1.7 %collective-permute-done.10 = f32[1,4,2,4,128]{4,3,2,1,0:T(4,128)S(1)} collective-permute-done((f32[1,4,2,4,128]{4,3,2,1,0:T(4,128)S(1)}, f32[1,4,2,4,128]{4,3,2,1,0:T(4,128)S(1)}, u32[]{:S(2)}, u32[]{:S(2)}) %collective-permute-start.10) | collective-permute-done | bytes 16416 | tf_op jit(solution)/shard_map/ppermute | solution.py:34
  44.4 1.9 %collective-permute-done.9 = f32[1,4,2,4,128]{4,3,2,1,0:T(4,128)S(1)} collective-permute-done((f32[1,4,2,4,128]{4,3,2,1,0:T(4,128)S(1)}, f32[1,4,2,4,128]{4,3,2,1,0:T(4,128)S(1)}, u32[]{:S(2)}, u32[]{:S(2)}) %collective-permute-start.9) | collective-permute-done | bytes 16416 | tf_op jit(solution)/shard_map/ppermute | solution.py:33
  46.3 0.1 collective-permute-start.12
  46.4 2.0 %collective-permute-start.11 = (f32[3,4,2,4,128]{4,3,2,1,0:T(4,128)S(1)}, f32[3,4,2,4,128]{4,3,2,1,0:T(4,128)S(1)}, u32[]{:S(2)}, u32[]{:S(2)}) collective-permute-start(f32[3,4,2,4,128]{4,3,2,1,0:T(4,128)S(1)} %pad_maximum_fusion.4), channel_id=1, source_target_pairs={{0,1},{1,2},{2,3},{3,0},{4,5},{5,6},{6,7},{7,4},{8,9},{9,10},{10,1... | collective-permute-start | bytes 147464 | tf_op jit(solution)/shard_map/ppermute | solution.py:33
  48.4 2.2 %collective-permute-done.12 = f32[3,4,2,4,128]{4,3,2,1,0:T(4,128)S(1)} collective-permute-done((f32[3,4,2,4,128]{4,3,2,1,0:T(4,128)S(1)}, f32[3,4,2,4,128]{4,3,2,1,0:T(4,128)S(1)}, u32[]{:S(2)}, u32[]{:S(2)}) %collective-permute-start.12) | collective-permute-done | bytes 49184 | tf_op jit(solution)/shard_map/ppermute | solution.py:34
  50.6 1.7 %collective-permute-done.11 = f32[3,4,2,4,128]{4,3,2,1,0:T(4,128)S(1)} collective-permute-done((f32[3,4,2,4,128]{4,3,2,1,0:T(4,128)S(1)}, f32[3,4,2,4,128]{4,3,2,1,0:T(4,128)S(1)}, u32[]{:S(2)}, u32[]{:S(2)}) %collective-permute-start.11) | collective-permute-done | bytes 49184 | tf_op jit(solution)/shard_map/ppermute | solution.py:33
  52.4 0.7 pad.11.feat_ref
  53.1 4.4 %density.4 = f32[8,128]{1,0:T(8,128)} custom-call(f32[72,8,128]{2,1,0:T(8,128)} %pad.11.feat_ref), custom_call_target="tpu_custom_call" | custom-call | tf_op jit(solution)/shard_map/density/pallas_call | solution.py:229
  57.5 1.4 %collective-permute-done.13 = f32[1,2,4,128]{3,2,1,0:T(4,128)S(1)} collective-permute-done((f32[1,2,4,128]{3,2,1,0:T(4,128)}, f32[1,2,4,128]{3,2,1,0:T(4,128)S(1)}, u32[]{:S(2)}, u32[]{:S(2)}) %collective-permute-start.13) | collective-permute-done | bytes 4128 | tf_op jit(solution)/shard_map/ppermute | solution.py:24
  58.9 0.3 collective-permute-start.15
  59.1 1.8 %collective-permute-start.14 = (f32[1,4,4,128]{3,2,1,0:T(4,128)S(1)}, f32[1,4,4,128]{3,2,1,0:T(4,128)S(1)}, u32[]{:S(2)}, u32[]{:S(2)}) collective-permute-start(f32[1,4,4,128]{3,2,1,0:T(4,128)S(1)} %pad_maximum_fusion.14), channel_id=1, source_target_pairs={{0,8},{8,16},{16,24},{24,0},{1,9},{9,17},{17,25},{25,1},{2,10},{10... | collective-permute-start | bytes 24584 | tf_op jit(solution)/shard_map/ppermute | solution.py:33
  60.9 1.6 %collective-permute-done.15 = f32[1,4,4,128]{3,2,1,0:T(4,128)S(1)} collective-permute-done((f32[1,4,4,128]{3,2,1,0:T(4,128)S(1)}, f32[1,4,4,128]{3,2,1,0:T(4,128)S(1)}, u32[]{:S(2)}, u32[]{:S(2)}) %collective-permute-start.15) | collective-permute-done | bytes 8224 | tf_op jit(solution)/shard_map/ppermute | solution.py:34
  62.6 1.1 %collective-permute-done.14 = f32[1,4,4,128]{3,2,1,0:T(4,128)S(1)} collective-permute-done((f32[1,4,4,128]{3,2,1,0:T(4,128)S(1)}, f32[1,4,4,128]{3,2,1,0:T(4,128)S(1)}, u32[]{:S(2)}, u32[]{:S(2)}) %collective-permute-start.14) | collective-permute-done | bytes 8224 | tf_op jit(solution)/shard_map/ppermute | solution.py:33
  63.7 0.6 pad_maximum_fusion.7
  64.3 5.7 %force_middle.1 = (f32[4,3,128]{2,1,0:T(4,128)}, f32[4,4,128]{2,1,0:T(4,128)}) custom-call(f32[72,8,128]{2,1,0:T(8,128)} %pad.11.feat_ref, f32[48,128]{1,0:T(8,128)} %bitcast.35, f32[4,3,128]{2,1,0:T(4,128)} %get-tuple-element.7.vel_ref), custom_call_target="tpu_custom_call" | custom-call | tf_op jit(solution)/shard_map/force_middle/pallas_call | solution.py:243
  70.0 1.4 %collective-permute-done.16 = f32[1,2,2,4,128]{4,3,2,1,0:T(4,128)S(1)} collective-permute-done((f32[1,2,2,4,128]{4,3,2,1,0:T(4,128)}, f32[1,2,2,4,128]{4,3,2,1,0:T(4,128)S(1)}, u32[]{:S(2)}, u32[]{:S(2)}) %collective-permute-start.16) | collective-permute-done | bytes 8224 | tf_op jit(solution)/shard_map/ppermute | solution.py:24
  71.4 1.9 %collective-permute-start.18 = (f32[1,4,2,4,128]{4,3,2,1,0:T(4,128)S(1)}, f32[1,4,2,4,128]{4,3,2,1,0:T(4,128)S(1)}, u32[]{:S(2)}, u32[]{:S(2)}) collective-permute-start(f32[1,4,2,4,128]{4,3,2,1,0:T(4,128)S(1)} %pad_maximum_fusion.11), channel_id=1, source_target_pairs={{8,0},{16,8},{24,16},{0,24},{9,1},{17,9},{25,17},{1,25},{10,2},{18... | collective-permute-start | bytes 49160 | tf_op jit(solution)/shard_map/ppermute | solution.py:34
  73.3 0.2 collective-permute-start.17
  73.5 1.7 %collective-permute-done.18 = f32[1,4,2,4,128]{4,3,2,1,0:T(4,128)S(1)} collective-permute-done((f32[1,4,2,4,128]{4,3,2,1,0:T(4,128)S(1)}, f32[1,4,2,4,128]{4,3,2,1,0:T(4,128)S(1)}, u32[]{:S(2)}, u32[]{:S(2)}) %collective-permute-start.18) | collective-permute-done | bytes 16416 | tf_op jit(solution)/shard_map/ppermute | solution.py:34
  75.2 2.7 %collective-permute-done.17 = f32[1,4,2,4,128]{4,3,2,1,0:T(4,128)S(1)} collective-permute-done((f32[1,4,2,4,128]{4,3,2,1,0:T(4,128)S(1)}, f32[1,4,2,4,128]{4,3,2,1,0:T(4,128)S(1)}, u32[]{:S(2)}, u32[]{:S(2)}) %collective-permute-start.17) | collective-permute-done | bytes 16416 | tf_op jit(solution)/shard_map/ppermute | solution.py:33
  77.9 0.1 collective-permute-start.20
  78.0 2.0 %collective-permute-start.19 = (f32[3,4,2,4,128]{4,3,2,1,0:T(4,128)S(1)}, f32[3,4,2,4,128]{4,3,2,1,0:T(4,128)S(1)}, u32[]{:S(2)}, u32[]{:S(2)}) collective-permute-start(f32[3,4,2,4,128]{4,3,2,1,0:T(4,128)S(1)} %pad_maximum_fusion.5), channel_id=1, source_target_pairs={{0,1},{1,2},{2,3},{3,0},{4,5},{5,6},{6,7},{7,4},{8,9},{9,10},{10,1... | collective-permute-start | bytes 147464 | tf_op jit(solution)/shard_map/ppermute | solution.py:33
  80.0 2.3 %collective-permute-done.20 = f32[3,4,2,4,128]{4,3,2,1,0:T(4,128)S(1)} collective-permute-done((f32[3,4,2,4,128]{4,3,2,1,0:T(4,128)S(1)}, f32[3,4,2,4,128]{4,3,2,1,0:T(4,128)S(1)}, u32[]{:S(2)}, u32[]{:S(2)}) %collective-permute-start.20) | collective-permute-done | bytes 49184 | tf_op jit(solution)/shard_map/ppermute | solution.py:34
  82.3 1.6 %collective-permute-done.19 = f32[3,4,2,4,128]{4,3,2,1,0:T(4,128)S(1)} collective-permute-done((f32[3,4,2,4,128]{4,3,2,1,0:T(4,128)S(1)}, f32[3,4,2,4,128]{4,3,2,1,0:T(4,128)S(1)}, u32[]{:S(2)}, u32[]{:S(2)}) %collective-permute-start.19) | collective-permute-done | bytes 49184 | tf_op jit(solution)/shard_map/ppermute | solution.py:33
  84.0 0.7 pad.12.feat_ref
  84.7 4.4 %density.5 = f32[8,128]{1,0:T(8,128)} custom-call(f32[72,8,128]{2,1,0:T(8,128)} %pad.12.feat_ref), custom_call_target="tpu_custom_call" | custom-call | tf_op jit(solution)/shard_map/density/pallas_call | solution.py:229
  89.1 0.0 collective-permute-start.21
  89.1 1.4 %collective-permute-done.21 = f32[1,2,4,128]{3,2,1,0:T(4,128)S(1)} collective-permute-done((f32[1,2,4,128]{3,2,1,0:T(4,128)}, f32[1,2,4,128]{3,2,1,0:T(4,128)S(1)}, u32[]{:S(2)}, u32[]{:S(2)}) %collective-permute-start.21) | collective-permute-done | bytes 4128 | tf_op jit(solution)/shard_map/ppermute | solution.py:24
  90.5 0.3 collective-permute-start.23
  90.8 1.8 %collective-permute-start.22 = (f32[1,4,4,128]{3,2,1,0:T(4,128)S(1)}, f32[1,4,4,128]{3,2,1,0:T(4,128)S(1)}, u32[]{:S(2)}, u32[]{:S(2)}) collective-permute-start(f32[1,4,4,128]{3,2,1,0:T(4,128)S(1)} %pad_maximum_fusion.15), channel_id=1, source_target_pairs={{0,8},{8,16},{16,24},{24,0},{1,9},{9,17},{17,25},{25,1},{2,10},{10... | collective-permute-start | bytes 24584 | tf_op jit(solution)/shard_map/ppermute | solution.py:33
  92.6 0.6 copy.14
  93.2 1.0 collective-permute-done.23
  94.2 1.1 %collective-permute-done.22 = f32[1,4,4,128]{3,2,1,0:T(4,128)S(1)} collective-permute-done((f32[1,4,4,128]{3,2,1,0:T(4,128)S(1)}, f32[1,4,4,128]{3,2,1,0:T(4,128)S(1)}, u32[]{:S(2)}, u32[]{:S(2)}) %collective-permute-start.22) | collective-permute-done | bytes 8224 | tf_op jit(solution)/shard_map/ppermute | solution.py:33
  95.3 0.6 pad_maximum_fusion.8
  95.9 5.8 %force_last.1 = f32[4,3,128]{2,1,0:T(4,128)} custom-call(f32[72,8,128]{2,1,0:T(8,128)} %pad.12.feat_ref, f32[48,128]{1,0:T(8,128)} %bitcast.41, f32[4,3,128]{2,1,0:T(4,128)} %get-tuple-element.9.vel_ref), custom_call_target="tpu_custom_call" | custom-call | tf_op jit(solution)/shard_map/force_last/pallas_call | solution.py:243
  101.7 1.3 %copy.15 = f32[1,2,2,3,128]{4,2,1,0,3:T(2,128)} copy(f32[1,2,2,3,128]{4,3,2,1,0:T(4,128)} %bitcast.56) | data formatting | bytes 12288 | tf_op jit(solution)/shard_map/reshape | solution.py:262
  (36 shorter events, 0.2 us)
Async XLA Ops:
  0.6 0.7 copy-start.7
  0.6 1.4 %copy-start.1 = (f32[3,1,2,2,128]{4,3,2,1,0:T(2,128)S(1)}, f32[3,1,2,2,128]{4,3,2,1,0:T(2,128)}, u32[]{:S(2)}) copy-start(f32[3,1,2,2,128]{4,3,2,1,0:T(2,128)} %param.4) | copy-start | bytes 18436
  2.1 1.4 %collective-permute-start = (f32[1,2,2,4,128]{4,2,1,0,3:T(2,128)S(1)}, f32[1,2,2,4,128]{4,2,1,0,3:T(2,128)S(1)}, u32[]{:S(2)}, u32[]{:S(2)}) collective-permute-start(f32[1,2,2,4,128]{4,2,1,0,3:T(2,128)S(1)} %pad_maximum_fusion.12), channel_id=1, source_target_pairs={{0,4},{4,0},{1,5},{5,1},{2,6},{6,2},{3,7},{7,3},{8,12},{12,8},{9,1... | collective-permute-start | bytes 24584 | tf_op jit(solution)/shard_map/ppermute | solution.py:24
  3.5 5.3 %collective-permute-start.2 = (f32[1,4,2,4,128]{4,2,1,0,3:T(2,128)S(1)}, f32[1,4,2,4,128]{4,2,1,0,3:T(2,128)S(1)}, u32[]{:S(2)}, u32[]{:S(2)}) collective-permute-start(f32[1,4,2,4,128]{4,2,1,0,3:T(2,128)S(1)} %pad_maximum_fusion.9), channel_id=1, source_target_pairs={{8,0},{16,8},{24,16},{0,24},{9,1},{17,9},{25,17},{1,25},{10,2},{18... | collective-permute-start | bytes 49160 | tf_op jit(solution)/shard_map/ppermute | solution.py:34
  7.3 4.6 %collective-permute-start.1 = (f32[1,4,2,4,128]{4,2,1,0,3:T(2,128)S(1)}, f32[1,4,2,4,128]{4,2,1,0,3:T(2,128)S(1)}, u32[]{:S(2)}, u32[]{:S(2)}) collective-permute-start(f32[1,4,2,4,128]{4,2,1,0,3:T(2,128)S(1)} %pad_maximum_fusion.9), channel_id=1, source_target_pairs={{0,8},{8,16},{16,24},{24,0},{1,9},{9,17},{17,25},{25,1},{2,10},{10... | collective-permute-start | bytes 49160 | tf_op jit(solution)/shard_map/ppermute | solution.py:33
  12.0 5.4 %collective-permute-start.4 = (f32[3,4,2,4,128]{4,2,1,0,3:T(2,128)S(1)}, f32[3,4,2,4,128]{4,2,1,0,3:T(2,128)S(1)}, u32[]{:S(2)}, u32[]{:S(2)}) collective-permute-start(f32[3,4,2,4,128]{4,2,1,0,3:T(2,128)S(1)} %pad_maximum_fusion.3), channel_id=1, source_target_pairs={{1,0},{2,1},{3,2},{0,3},{5,4},{6,5},{7,6},{4,7},{9,8},{10,9},{11,1... | collective-permute-start | bytes 147464 | tf_op jit(solution)/shard_map/ppermute | solution.py:34
  15.6 5.9 %collective-permute-start.3 = (f32[3,4,2,4,128]{4,2,1,0,3:T(2,128)S(1)}, f32[3,4,2,4,128]{4,2,1,0,3:T(2,128)S(1)}, u32[]{:S(2)}, u32[]{:S(2)}) collective-permute-start(f32[3,4,2,4,128]{4,2,1,0,3:T(2,128)S(1)} %pad_maximum_fusion.3), channel_id=1, source_target_pairs={{0,1},{1,2},{2,3},{3,0},{4,5},{5,6},{6,7},{7,4},{8,9},{9,10},{10,1... | collective-permute-start | bytes 147464 | tf_op jit(solution)/shard_map/ppermute | solution.py:33
  26.8 1.4 %copy-start.4 = (f32[8,128]{1,0:T(8,128)S(1)}, f32[8,128]{1,0:T(8,128)}, u32[]{:S(2)}) copy-start(f32[8,128]{1,0:T(8,128)} %density.3) | copy-start | bytes 12292
  26.8 1.4 %collective-permute-start.5 = (f32[1,2,4,128]{3,2,1,0:T(4,128)}, f32[1,2,4,128]{3,2,1,0:T(4,128)S(1)}, u32[]{:S(2)}, u32[]{:S(2)}) collective-permute-start(f32[1,2,4,128]{3,2,1,0:T(4,128)} %bitcast.49), channel_id=1, source_target_pairs={{0,4},{4,0},{1,5},{5,1},{2,6},{6,2},{3,7},{7,3},{8,12},{12,8},{9,1... | collective-permute-start | bytes 12296 | tf_op jit(solution)/shard_map/ppermute | solution.py:24
  28.2 2.1 %copy-start.6 = (f32[3,1,2,2,128]{4,3,2,1,0:T(2,128)S(1)}, f32[3,1,2,2,128]{4,3,2,1,0:T(2,128)}, u32[]{:S(2)}) copy-start(f32[3,1,2,2,128]{4,3,2,1,0:T(2,128)} %param.5) | copy-start | bytes 18436
  28.2 3.7 %collective-permute-start.7 = (f32[1,4,4,128]{3,2,1,0:T(4,128)S(1)}, f32[1,4,4,128]{3,2,1,0:T(4,128)S(1)}, u32[]{:S(2)}, u32[]{:S(2)}) collective-permute-start(f32[1,4,4,128]{3,2,1,0:T(4,128)S(1)} %pad_maximum_fusion.13), channel_id=1, source_target_pairs={{8,0},{16,8},{24,16},{0,24},{9,1},{17,9},{25,17},{1,25},{10,2},{18... | collective-permute-start | bytes 24584 | tf_op jit(solution)/shard_map/ppermute | solution.py:34
  28.3 4.6 %collective-permute-start.6 = (f32[1,4,4,128]{3,2,1,0:T(4,128)S(1)}, f32[1,4,4,128]{3,2,1,0:T(4,128)S(1)}, u32[]{:S(2)}, u32[]{:S(2)}) collective-permute-start(f32[1,4,4,128]{3,2,1,0:T(4,128)S(1)} %pad_maximum_fusion.13), channel_id=1, source_target_pairs={{0,8},{8,16},{16,24},{24,0},{1,9},{9,17},{17,25},{25,1},{2,10},{10... | collective-permute-start | bytes 24584 | tf_op jit(solution)/shard_map/ppermute | solution.py:33
  39.2 1.4 %copy-start.2 = (f32[4,4,128]{2,1,0:T(4,128)S(1)}, f32[4,4,128]{2,1,0:T(4,128)}, u32[]{:S(2)}) copy-start(f32[4,4,128]{2,1,0:T(4,128)} %get-tuple-element.6) | copy-start | bytes 24580
  39.2 1.4 %collective-permute-start.8 = (f32[1,2,2,4,128]{4,3,2,1,0:T(4,128)}, f32[1,2,2,4,128]{4,3,2,1,0:T(4,128)S(1)}, u32[]{:S(2)}, u32[]{:S(2)}) collective-permute-start(f32[1,2,2,4,128]{4,3,2,1,0:T(4,128)} %bitcast.42), channel_id=1, source_target_pairs={{0,4},{4,0},{1,5},{5,1},{2,6},{6,2},{3,7},{7,3},{8,12},{12,8},{9,1... | collective-permute-start | bytes 24584 | tf_op jit(solution)/shard_map/ppermute | solution.py:24
  40.6 3.8 %collective-permute-start.10 = (f32[1,4,2,4,128]{4,3,2,1,0:T(4,128)S(1)}, f32[1,4,2,4,128]{4,3,2,1,0:T(4,128)S(1)}, u32[]{:S(2)}, u32[]{:S(2)}) collective-permute-start(f32[1,4,2,4,128]{4,3,2,1,0:T(4,128)S(1)} %pad_maximum_fusion.10), channel_id=1, source_target_pairs={{8,0},{16,8},{24,16},{0,24},{9,1},{17,9},{25,17},{1,25},{10,2},{18... | collective-permute-start | bytes 49160 | tf_op jit(solution)/shard_map/ppermute | solution.py:34
  41.7 4.6 %collective-permute-start.9 = (f32[1,4,2,4,128]{4,3,2,1,0:T(4,128)S(1)}, f32[1,4,2,4,128]{4,3,2,1,0:T(4,128)S(1)}, u32[]{:S(2)}, u32[]{:S(2)}) collective-permute-start(f32[1,4,2,4,128]{4,3,2,1,0:T(4,128)S(1)} %pad_maximum_fusion.10), channel_id=1, source_target_pairs={{0,8},{8,16},{16,24},{24,0},{1,9},{9,17},{17,25},{25,1},{2,10},{10... | collective-permute-start | bytes 49160 | tf_op jit(solution)/shard_map/ppermute | solution.py:33
  46.3 4.3 %collective-permute-start.12 = (f32[3,4,2,4,128]{4,3,2,1,0:T(4,128)S(1)}, f32[3,4,2,4,128]{4,3,2,1,0:T(4,128)S(1)}, u32[]{:S(2)}, u32[]{:S(2)}) collective-permute-start(f32[3,4,2,4,128]{4,3,2,1,0:T(4,128)S(1)} %pad_maximum_fusion.4), channel_id=1, source_target_pairs={{1,0},{2,1},{3,2},{0,3},{5,4},{6,5},{7,6},{4,7},{9,8},{10,9},{11,1... | collective-permute-start | bytes 147464 | tf_op jit(solution)/shard_map/ppermute | solution.py:34
  46.4 5.9 %collective-permute-start.11 = (f32[3,4,2,4,128]{4,3,2,1,0:T(4,128)S(1)}, f32[3,4,2,4,128]{4,3,2,1,0:T(4,128)S(1)}, u32[]{:S(2)}, u32[]{:S(2)}) collective-permute-start(f32[3,4,2,4,128]{4,3,2,1,0:T(4,128)S(1)} %pad_maximum_fusion.4), channel_id=1, source_target_pairs={{0,1},{1,2},{2,3},{3,0},{4,5},{5,6},{6,7},{7,4},{8,9},{9,10},{10,1... | collective-permute-start | bytes 147464 | tf_op jit(solution)/shard_map/ppermute | solution.py:33
  57.5 1.4 %copy-start.5 = (f32[8,128]{1,0:T(8,128)S(1)}, f32[8,128]{1,0:T(8,128)}, u32[]{:S(2)}) copy-start(f32[8,128]{1,0:T(8,128)} %density.4) | copy-start | bytes 12292
  57.5 1.4 %collective-permute-start.13 = (f32[1,2,4,128]{3,2,1,0:T(4,128)}, f32[1,2,4,128]{3,2,1,0:T(4,128)S(1)}, u32[]{:S(2)}, u32[]{:S(2)}) collective-permute-start(f32[1,2,4,128]{3,2,1,0:T(4,128)} %bitcast.52), channel_id=1, source_target_pairs={{0,4},{4,0},{1,5},{5,1},{2,6},{6,2},{3,7},{7,3},{8,12},{12,8},{9,1... | collective-permute-start | bytes 12296 | tf_op jit(solution)/shard_map/ppermute | solution.py:24
  58.9 3.7 %collective-permute-start.15 = (f32[1,4,4,128]{3,2,1,0:T(4,128)S(1)}, f32[1,4,4,128]{3,2,1,0:T(4,128)S(1)}, u32[]{:S(2)}, u32[]{:S(2)}) collective-permute-start(f32[1,4,4,128]{3,2,1,0:T(4,128)S(1)} %pad_maximum_fusion.14), channel_id=1, source_target_pairs={{8,0},{16,8},{24,16},{0,24},{9,1},{17,9},{25,17},{1,25},{10,2},{18... | collective-permute-start | bytes 24584 | tf_op jit(solution)/shard_map/ppermute | solution.py:34
  59.1 4.6 %collective-permute-start.14 = (f32[1,4,4,128]{3,2,1,0:T(4,128)S(1)}, f32[1,4,4,128]{3,2,1,0:T(4,128)S(1)}, u32[]{:S(2)}, u32[]{:S(2)}) collective-permute-start(f32[1,4,4,128]{3,2,1,0:T(4,128)S(1)} %pad_maximum_fusion.14), channel_id=1, source_target_pairs={{0,8},{8,16},{16,24},{24,0},{1,9},{9,17},{17,25},{25,1},{2,10},{10... | collective-permute-start | bytes 24584 | tf_op jit(solution)/shard_map/ppermute | solution.py:33
  70.0 1.4 %copy-start = (f32[4,4,128]{2,1,0:T(4,128)S(1)}, f32[4,4,128]{2,1,0:T(4,128)}, u32[]{:S(2)}) copy-start(f32[4,4,128]{2,1,0:T(4,128)} %get-tuple-element.8) | copy-start | bytes 24580
  70.0 1.4 %collective-permute-start.16 = (f32[1,2,2,4,128]{4,3,2,1,0:T(4,128)}, f32[1,2,2,4,128]{4,3,2,1,0:T(4,128)S(1)}, u32[]{:S(2)}, u32[]{:S(2)}) collective-permute-start(f32[1,2,2,4,128]{4,3,2,1,0:T(4,128)} %bitcast.30), channel_id=1, source_target_pairs={{0,4},{4,0},{1,5},{5,1},{2,6},{6,2},{3,7},{7,3},{8,12},{12,8},{9,1... | collective-permute-start | bytes 24584 | tf_op jit(solution)/shard_map/ppermute | solution.py:24
  71.4 3.8 %collective-permute-start.18 = (f32[1,4,2,4,128]{4,3,2,1,0:T(4,128)S(1)}, f32[1,4,2,4,128]{4,3,2,1,0:T(4,128)S(1)}, u32[]{:S(2)}, u32[]{:S(2)}) collective-permute-start(f32[1,4,2,4,128]{4,3,2,1,0:T(4,128)S(1)} %pad_maximum_fusion.11), channel_id=1, source_target_pairs={{8,0},{16,8},{24,16},{0,24},{9,1},{17,9},{25,17},{1,25},{10,2},{18... | collective-permute-start | bytes 49160 | tf_op jit(solution)/shard_map/ppermute | solution.py:34
  73.3 4.6 %collective-permute-start.17 = (f32[1,4,2,4,128]{4,3,2,1,0:T(4,128)S(1)}, f32[1,4,2,4,128]{4,3,2,1,0:T(4,128)S(1)}, u32[]{:S(2)}, u32[]{:S(2)}) collective-permute-start(f32[1,4,2,4,128]{4,3,2,1,0:T(4,128)S(1)} %pad_maximum_fusion.11), channel_id=1, source_target_pairs={{0,8},{8,16},{16,24},{24,0},{1,9},{9,17},{17,25},{25,1},{2,10},{10... | collective-permute-start | bytes 49160 | tf_op jit(solution)/shard_map/ppermute | solution.py:33
  77.9 4.4 %collective-permute-start.20 = (f32[3,4,2,4,128]{4,3,2,1,0:T(4,128)S(1)}, f32[3,4,2,4,128]{4,3,2,1,0:T(4,128)S(1)}, u32[]{:S(2)}, u32[]{:S(2)}) collective-permute-start(f32[3,4,2,4,128]{4,3,2,1,0:T(4,128)S(1)} %pad_maximum_fusion.5), channel_id=1, source_target_pairs={{1,0},{2,1},{3,2},{0,3},{5,4},{6,5},{7,6},{4,7},{9,8},{10,9},{11,1... | collective-permute-start | bytes 147464 | tf_op jit(solution)/shard_map/ppermute | solution.py:34
  78.0 5.9 %collective-permute-start.19 = (f32[3,4,2,4,128]{4,3,2,1,0:T(4,128)S(1)}, f32[3,4,2,4,128]{4,3,2,1,0:T(4,128)S(1)}, u32[]{:S(2)}, u32[]{:S(2)}) collective-permute-start(f32[3,4,2,4,128]{4,3,2,1,0:T(4,128)S(1)} %pad_maximum_fusion.5), channel_id=1, source_target_pairs={{0,1},{1,2},{2,3},{3,0},{4,5},{5,6},{6,7},{7,4},{8,9},{9,10},{10,1... | collective-permute-start | bytes 147464 | tf_op jit(solution)/shard_map/ppermute | solution.py:33
  89.1 1.4 %copy-start.3 = (f32[8,128]{1,0:T(8,128)S(1)}, f32[8,128]{1,0:T(8,128)}, u32[]{:S(2)}) copy-start(f32[8,128]{1,0:T(8,128)} %density.5) | copy-start | bytes 12292
  89.1 1.4 %collective-permute-start.21 = (f32[1,2,4,128]{3,2,1,0:T(4,128)}, f32[1,2,4,128]{3,2,1,0:T(4,128)S(1)}, u32[]{:S(2)}, u32[]{:S(2)}) collective-permute-start(f32[1,2,4,128]{3,2,1,0:T(4,128)} %bitcast.46), channel_id=1, source_target_pairs={{0,4},{4,0},{1,5},{5,1},{2,6},{6,2},{3,7},{7,3},{8,12},{12,8},{9,1... | collective-permute-start | bytes 12296 | tf_op jit(solution)/shard_map/ppermute | solution.py:24
  90.5 3.7 %collective-permute-start.23 = (f32[1,4,4,128]{3,2,1,0:T(4,128)S(1)}, f32[1,4,4,128]{3,2,1,0:T(4,128)S(1)}, u32[]{:S(2)}, u32[]{:S(2)}) collective-permute-start(f32[1,4,4,128]{3,2,1,0:T(4,128)S(1)} %pad_maximum_fusion.15), channel_id=1, source_target_pairs={{8,0},{16,8},{24,16},{0,24},{9,1},{17,9},{25,17},{1,25},{10,2},{18... | collective-permute-start | bytes 24584 | tf_op jit(solution)/shard_map/ppermute | solution.py:34
  90.8 4.5 %collective-permute-start.22 = (f32[1,4,4,128]{3,2,1,0:T(4,128)S(1)}, f32[1,4,4,128]{3,2,1,0:T(4,128)S(1)}, u32[]{:S(2)}, u32[]{:S(2)}) collective-permute-start(f32[1,4,4,128]{3,2,1,0:T(4,128)S(1)} %pad_maximum_fusion.15), channel_id=1, source_target_pairs={{0,8},{8,16},{16,24},{24,0},{1,9},{9,17},{17,25},{25,1},{2,10},{10... | collective-permute-start | bytes 24584 | tf_op jit(solution)/shard_map/ppermute | solution.py:33
where the time goes:
time: 103 us
  waiting for transfers between devices  41.1 us (40%)
  Pallas kernels  30.3 us (29%)
  starting transfers between devices  22.6 us (22%)
  local copies, waits for them, and re-layouts  5.49 us (5%)
  other arithmetic  2.8 us (3%)
    ppermute x9, waiting for transfers between devices, ring_halo(): lax.ppermute(tail, axis, [(i, (i + 1) % count) for i in range(count)])  18.5 us
    pallas_call x3, Pallas kernels, evaluate(): pl.pallas_call(functools.partial(force_kernel, extent, stage), out_shape=...  17.2 us
    ppermute x9, waiting for transfers between devices, ring_halo(): lax.ppermute(head, axis, [((i + 1) % count, i) for i in range(count)])  14.8 us
    pallas_call x3, Pallas kernels, evaluate(): pl.pallas_call(functools.partial(density_kernel, extent), out_shape=jax.S...  13.1 us
    ppermute x9, starting transfers between devices, ring_halo(): lax.ppermute(head, axis, [((i + 1) % count, i) for i in range(count)])  11.2 us
    ppermute x9, starting transfers between devices, ring_halo(): lax.ppermute(tail, axis, [(i, (i + 1) % count) for i in range(count)])  10.8 us
    ppermute x6, waiting for transfers between devices, ring_halo(): other = lax.ppermute(cells, axis, [(0, 1), (1, 0)])  7.71 us
    pad x3, local copies, waits for them, and re-layouts, evaluate(): feat = jnp.pad(wide.reshape(cells, 4, slots), ((0, 0), (0, 4), (0, 0)))  2.21 us
  transfers between devices with their start and end apart: 24, of which 24 were waited for; matrix products, arithmetic and copies ran while one was open for 1% of the time, Pallas kernels for 0%

commit v1 on v0

v1 whole, which is shorter than its diff:
```python
import functools

import jax
import jax.numpy as jnp
from jax import lax
from jax.experimental import pallas as pl
from jax.experimental.pallas import tpu as pltpu
from jax.sharding import PartitionSpec as P

time_step = 0.05
half_kick = 0.5 * time_step
LANES = 128
GRANT = 8 * 1024 * 1024
ROOT = 1.3 ** (1.0 / 3.0)


def ring_halo(cells, axis, dim, width):
    count = lax.axis_size(axis)
    size = cells.shape[dim]
    head = lax.slice_in_dim(cells, 0, width, axis=dim)
    tail = lax.slice_in_dim(cells, size - width, size, axis=dim)
    if count == 1:
        return jnp.concatenate([tail, cells, head], axis=dim)
    if count == 2 and size == 2 * width:
        other = lax.ppermute(cells, axis, [(0, 1), (1, 0)])
        return jnp.concatenate(
            [
                lax.slice_in_dim(other, width, size, axis=dim),
                cells,
                lax.slice_in_dim(other, 0, width, axis=dim),
            ],
            axis=dim,
        )
    below = lax.ppermute(tail, axis, [(i, (i + 1) % count) for i in range(count)])
    above = lax.ppermute(head, axis, [((i + 1) % count, i) for i in range(count)])
    return jnp.concatenate([below, cells, above], axis=dim)


def by_code(code, first, second):
    return jnp.where(code > 1.5, second, jnp.where(code > 0.5, first, 0.0))


def split3(value):
    high = value.astype(jnp.bfloat16).astype(jnp.float32)
    rest = value - high
    middle = rest.astype(jnp.bfloat16).astype(jnp.float32)
    return high, middle, rest - middle


def row_masks():
    row = lax.broadcasted_iota(jnp.int32, (8, LANES), 0)
    masks = [(row == k).astype(jnp.float32) for k in range(7)]
    return masks, masks[0] + masks[1] + masks[2]


def placed(tile, centre, masks, spatial):
    point = tile * spatial
    for axis in range(3):
        if centre[axis]:
            point = point + centre[axis] * masks[axis]
    return point, jnp.sum(point * point, axis=0, keepdims=True)


def partner_block(row):
    high, middle, low = split3(row)
    first = jnp.concatenate([high, middle], axis=0).astype(jnp.bfloat16)
    last = jnp.concatenate([low, high], axis=0).astype(jnp.bfloat16)
    return jnp.concatenate([first, first, last], axis=0)


def target_block(row):
    high, middle, low = split3(row)
    stacked = jnp.concatenate([high, high, middle, middle, high, low], axis=0)
    return jnp.transpose(stacked).astype(jnp.bfloat16)


def centre_of(cell, extent):
    return tuple(float(c) - 0.5 * e for c, e in zip(cell, extent))


def density_kernel(extent, feat_ref, slope_ref, part_ref):
    ex, ey, ez = extent
    masks, spatial = row_masks()
    for a in range(ex):
        for b in range(ey):
            for c in range(ez):
                index = (a * ey + b) * ez + c
                tile = feat_ref[index]
                point, norm = placed(tile, centre_of((a, b, c), extent), masks, spatial)
                scale = by_code(tile[3:4], 1.0, ROOT)
                part_ref[:, index * LANES : (index + 1) * LANES] = partner_block(
                    (point - norm * masks[3] + masks[4]) * scale
                )
    place = 0
    rows = 64
    for a in range(1, ex - 1):
        for b in range(1, ey - 1):
            for c in range(1, ez - 1):
                index = (a * ey + b) * ez + c
                tile = feat_ref[index]
                point, norm = placed(tile, centre_of((a, b, c), extent), masks, spatial)
                left = target_block(2.0 * point + masks[3] + (1.0 - norm) * masks[4])
                sums = []
                for start in range(0, LANES, rows):
                    total = jnp.zeros((rows, LANES), jnp.float32)
                    for p in (-1, 0, 1):
                        for q in (-1, 0, 1):
                            base = ((a + p) * ey + b + q) * ez + c - 1
                            near = jnp.dot(
                                left[start : start + rows],
                                part_ref[:, base * LANES : (base + 3) * LANES],
                                preferred_element_type=jnp.float32,
                            )
                            for k in range(3):
                                part = jnp.maximum(near[:, k * LANES : (k + 1) * LANES], 0.0)
                                if p == 0 and q == 0 and k == 1:
                                    i = lax.broadcasted_iota(jnp.int32, (rows, LANES), 0)
                                    j = lax.broadcasted_iota(jnp.int32, (rows, LANES), 1)
                                    part = jnp.where(i + start == j, 0.0, part)
                                total = total + part * part * part
                    sums.append(total)
                density = jnp.sum(jnp.transpose(jnp.concatenate(sums, axis=0)), axis=0, keepdims=True)
                present = by_code(tile[3:4], 1.0, 1.0)
                slope_ref[place : place + 1, :] = -0.5 * present / jnp.sqrt(density + 1.0)
                place += 1


def force_kernel(extent, stage, feat_ref, slope_ref, vel_ref, *refs):
    if stage == "first":
        new_vel_ref, new_loc_ref, part_ref, pair_ref, point_ref = refs
    elif stage == "middle":
        new_vel_ref, new_loc_ref, new_pos_ref, part_ref, pair_ref, point_ref = refs
    else:
        new_vel_ref, part_ref, pair_ref, point_ref = refs
    ex, ey, ez = extent
    near_z = ez - 2
    masks, spatial = row_masks()
    for a in range(ex):
        for b in range(ey):
            for c in range(near_z):
                index = (a * ey + b) * near_z + c
                lanes = slice(index * LANES, (index + 1) * LANES)
                tile = feat_ref[(a * ey + b) * ez + c + 1]
                point, norm = placed(tile, centre_of((a, b, c + 1), extent), masks, spatial)
                code = tile[3:4]
                scale = by_code(code, 0.6, 0.8)
                part_ref[:, lanes] = partner_block(
                    (point - norm * masks[3] + masks[4]) * scale
                )
                slope = slope_ref[index : index + 1, :]
                pair_ref[:, lanes] = partner_block(
                    by_code(code, 0.75 / 0.09, 0.75 * 1.3 / 0.16) * masks[5]
                    + slope * by_code(code, 0.75 / 0.09, 0.75 / 0.16) * masks[6]
                )
                point_ref[:, lanes] = point
    place = 0
    rows = 32
    for a in range(1, ex - 1):
        for b in range(1, ey - 1):
            for c in range(2, ez - 2):
                tile = feat_ref[(a * ey + b) * ez + c]
                point, norm = placed(tile, centre_of((a, b, c), extent), masks, spatial)
                code = tile[3:4]
                solute = code > 1.5
                index = (a * ey + b) * near_z + c - 1
                slope = slope_ref[index : index + 1, :]
                strength = jnp.where(solute, 0.4, 0.3)
                left = target_block(
                    (2.0 * point + masks[3] + (1.0 - norm) * masks[4]) * strength
                    + slope * jnp.where(solute, 1.0 / 0.16, 1.0 / 0.09) * masks[5]
                    + jnp.where(solute, 1.3 / 0.16, 1.0 / 0.09) * masks[6]
                )
                sums = [[] for _ in range(4)]
                for start in range(0, LANES, rows):
                    total = [jnp.zeros((rows, LANES), jnp.float32) for _ in range(4)]
                    for p in (-1, 0, 1):
                        for q in (-1, 0, 1):
                            base = ((a + p) * ey + b + q) * near_z + c - 2
                            span = slice(base * LANES, (base + 3) * LANES)
                            near = jnp.dot(
                                left[start : start + rows],
                                part_ref[:, span],
                                preferred_element_type=jnp.float32,
                            )
                            kappa = jnp.dot(
                                left[start : start + rows],
                                pair_ref[:, span],
                                preferred_element_type=jnp.float32,
                            )
                            for k in range(3):
                                lanes = slice((base + k) * LANES, (base + k + 1) * LANES)
                                s = jnp.maximum(near[:, k * LANES : (k + 1) * LANES], 0.0)
                                w = s * (1.0 + s * kappa[:, k * LANES : (k + 1) * LANES])
                                total[3] = total[3] + w
                                for axis in range(3):
                                    total[axis] = total[axis] + w * point_ref[axis : axis + 1, lanes]
                    for k in range(4):
                        sums[k].append(total[k])
                flat = [
                    jnp.sum(jnp.transpose(jnp.concatenate(parts, axis=0)), axis=0, keepdims=True)
                    for parts in sums
                ]
                present = by_code(code, 1.0, 1.0)
                kick = half_kick * jnp.where(solute, 1.6, 1.0)
                row = slice(place, place + 1)
                for axis in range(3):
                    force = -2.0 * present * (flat[axis] - point[axis : axis + 1] * flat[3])
                    speed = vel_ref[axis, row, :] + kick * force
                    if stage == "middle":
                        speed = speed + kick * force
                    new_vel_ref[axis, row, :] = speed
                    if stage != "last":
                        moved = tile[axis : axis + 1] + time_step * speed
                        new_loc_ref[place, axis : axis + 1, :] = moved
                        if stage == "middle":
                            new_pos_ref[axis, row, :] = moved
                if stage != "last":
                    new_loc_ref[place, 3:4, :] = code
                place += 1


def on_device(positions, velocities, species, counts):
    cx, cy, cz, slots = positions.shape[1:]
    present = lax.broadcasted_iota(jnp.int32, species.shape, 3) < counts[..., None]
    code = jnp.where(present, jnp.where(species == 1, 2.0, 1.0), 0.0)
    location = jnp.concatenate([jnp.moveaxis(positions, 0, 3), code[..., None, :]], axis=3)
    extent = (cx + 2, cy + 2, cz + 4)
    own = cx * cy * cz
    cells = extent[0] * extent[1] * extent[2]
    near = extent[0] * extent[1] * (cz + 2)
    velocity = velocities.reshape(3, own, slots)
    vmem = pl.BlockSpec(memory_space=pltpu.VMEM)
    flat_shape = jax.ShapeDtypeStruct((3, own, slots), jnp.float32)

    def evaluate(location, velocity, stage):
        wide = ring_halo(location, "gy", 1, 1)
        wide = ring_halo(wide, "gx", 0, 1)
        wide = ring_halo(wide, "gz", 2, 2)
        feat = jnp.pad(wide.reshape(cells, 4, slots), ((0, 0), (0, 4), (0, 0)))
        slopes = pl.pallas_call(
            functools.partial(density_kernel, extent),
            out_shape=jax.ShapeDtypeStruct((cx * cy * (cz + 2), slots), jnp.float32),
            in_specs=[vmem],
            out_specs=vmem,
            scratch_shapes=[pltpu.VMEM((48, cells * slots), jnp.bfloat16)],
            compiler_params=pltpu.CompilerParams(vmem_limit_bytes=GRANT),
            name="density",
        )(feat)
        slopes = slopes.reshape(cx, cy, cz + 2, slots)
        slopes = ring_halo(slopes, "gy", 1, 1)
        slopes = ring_halo(slopes, "gx", 0, 1).reshape(near, slots)
        out_shape = [flat_shape]
        if stage != "last":
            out_shape.append(jax.ShapeDtypeStruct((own, 4, slots), jnp.float32))
        if stage == "middle":
            out_shape.append(flat_shape)
        return pl.pallas_call(
            functools.partial(force_kernel, extent, stage),
            out_shape=out_shape,
            in_specs=[vmem] * 3,
            out_specs=[vmem] * len(out_shape),
            scratch_shapes=[
                pltpu.VMEM((48, near * slots), jnp.bfloat16),
                pltpu.VMEM((48, near * slots), jnp.bfloat16),
                pltpu.VMEM((8, near * slots), jnp.float32),
            ],
            compiler_params=pltpu.CompilerParams(vmem_limit_bytes=GRANT),
            name="force_" + stage,
        )(feat, slopes, velocity)

    velocity, moved = evaluate(location, velocity, "first")
    velocity, moved, new_positions = evaluate(moved.reshape(location.shape), velocity, "middle")
    (velocity,) = evaluate(moved.reshape(location.shape), velocity, "last")
    return new_positions.reshape(positions.shape), velocity.reshape(positions.shape)


def solution(mesh):
    return jax.shard_map(
        on_device,
        mesh=mesh,
        in_specs=(
            P(None, "gx", "gy", "gz", None),
            P(None, "gx", "gy", "gz", None),
            P("gx", "gy", "gz", None),
            P("gx", "gy", "gz"),
        ),
        out_specs=(P(None, "gx", "gy", "gz", None), P(None, "gx", "gy", "gz", None)),
        check_vma=False,
    )
```

time: 103 us -> 88.9 us (0.86)
  Pallas kernels: 30.3 us -> 21.3 us
  local copies, waits for them, and re-layouts: 5.49 us -> 1.53 us
  other arithmetic: 2.8 us -> 1.02 us
    pallas_call x3, Pallas kernels: 13.1 us -> 8.47 us  [evaluate(): pl.pallas_call(functools.partial(density_kernel, extent), out_shape=jax.S...]
    pallas_call x3, Pallas kernels: 17.2 us -> 12.8 us  [evaluate(): pl.pallas_call(functools.partial(force_kernel, extent, stage), out_shape=...]
    pad x3, local copies, waits for them, and re-layouts: 2.21 us -> 0.07 us  [evaluate(): feat = jnp.pad(wide.reshape(cells, 4, slots), ((0, 0), (0, 4), (0, 0)))]
    concatenate x9, other arithmetic: 2 us -> 0.21 us  [ring_halo(): return jnp.concatenate([below, cells, above], axis=dim)]
    reshape x1 -> x0, local copies, waits for them, and re-layouts: 1.29 us -> none  [on_device(): new_velocities = jnp.moveaxis(velocity.reshape(cx, cy, cz, 3, slots), 3, 0)]
    ppermute x9, waiting for transfers between devices: 14.8 us -> 16 us  [ring_halo(): lax.ppermute(head, axis, [((i + 1) % count, i) for i in range(count)])]
    ppermute x6, waiting for transfers between devices: 7.71 us -> 6.62 us  [ring_halo(): other = lax.ppermute(cells, axis, [(0, 1), (1, 0)])]
  transfers between devices with their start and end apart: 24 -> 24, of which waited for: 24 -> 24; matrix products, arithmetic and copies ran while one was open for 1% -> 0% of each run, Pallas kernels for 0% -> 0%
where the time goes in v1:
time: 88.9 us; the launch traced here: 88.7 us
  waiting for transfers between devices  41.2 us (46%)
  starting transfers between devices  22.8 us (26%)
  Pallas kernels  21.3 us (24%)
  local copies, waits for them, and re-layouts  1.53 us (2%)
  other arithmetic  1.02 us (1%)
    ppermute x9, waiting for transfers between devices, ring_halo(): lax.ppermute(tail, axis, [(i, (i + 1) % count) for i in range(count)])  18.5 us
    ppermute x9, waiting for transfers between devices, ring_halo(): lax.ppermute(head, axis, [((i + 1) % count, i) for i in range(count)])  16 us
    pallas_call x3, Pallas kernels, evaluate(): pl.pallas_call(functools.partial(force_kernel, extent, stage), out_shape=...  12.8 us
    ppermute x9, starting transfers between devices, ring_halo(): lax.ppermute(head, axis, [((i + 1) % count, i) for i in range(count)])  11.1 us
    ppermute x9, starting transfers between devices, ring_halo(): lax.ppermute(tail, axis, [(i, (i + 1) % count) for i in range(count)])  10.8 us
    pallas_call x3, Pallas kernels, evaluate(): pl.pallas_call(functools.partial(density_kernel, extent), out_shape=jax.S...  8.47 us
    ppermute x6, waiting for transfers between devices, ring_halo(): other = lax.ppermute(cells, axis, [(0, 1), (1, 0)])  6.62 us
  transfers between devices with their start and end apart: 24, of which 24 were waited for; matrix products, arithmetic and copies ran while one was open for 0% of the time, Pallas kernels for 0%

profile of v1, /device:TPU:0, one launch (start us, length us, event | category | flops | bytes accessed | tf_op | source)
XLA Modules:
  0.0 88.7 jit_solution(6289383014238672275)
XLA Ops:
  0.6 0.0 copy-start.2
  0.6 0.0 copy-start.1
  0.6 0.7 copy-done.2
  1.3 0.8 fusion
  2.1 0.0 copy-done.1
  2.1 0.6 collective-permute-start
  2.6 0.8 collective-permute-done
  3.5 3.8 %collective-permute-start.2 = (f32[1,4,2,4,128]{4,2,1,0,3:T(2,128)S(1)}, f32[1,4,2,4,128]{4,2,1,0,3:T(2,128)S(1)}, u32[]{:S(2)}, u32[]{:S(2)}) collective-permute-start(f32[1,4,2,4,128]{4,2,1,0,3:T(2,128)S(1)} %pad_maximum_fusion.9), channel_id=1, source_target_pairs={{8,0},{16,8},{24,16},{0,24},{9,1},{17,9},{25,17},{1,25},{10,2},{18... | collective-permute-start | bytes 49160 | tf_op jit(solution)/shard_map/ppermute | solution.py:35
  7.3 0.0 collective-permute-start.1
  7.3 1.4 %collective-permute-done.2 = f32[1,4,2,4,128]{4,2,1,0,3:T(2,128)S(1)} collective-permute-done((f32[1,4,2,4,128]{4,2,1,0,3:T(2,128)S(1)}, f32[1,4,2,4,128]{4,2,1,0,3:T(2,128)S(1)}, u32[]{:S(2)}, u32[]{:S(2)}) %collective-permute-start.2) | collective-permute-done | bytes 16416 | tf_op jit(solution)/shard_map/ppermute | solution.py:35
  8.7 3.2 %collective-permute-done.1 = f32[1,4,2,4,128]{4,2,1,0,3:T(2,128)S(1)} collective-permute-done((f32[1,4,2,4,128]{4,2,1,0,3:T(2,128)S(1)}, f32[1,4,2,4,128]{4,2,1,0,3:T(2,128)S(1)}, u32[]{:S(2)}, u32[]{:S(2)}) %collective-permute-start.1) | collective-permute-done | bytes 16416 | tf_op jit(solution)/shard_map/ppermute | solution.py:34
  12.0 3.7 %collective-permute-start.4 = (f32[3,4,2,4,128]{4,2,1,0,3:T(2,128)S(1)}, f32[3,4,2,4,128]{4,2,1,0,3:T(2,128)S(1)}, u32[]{:S(2)}, u32[]{:S(2)}) collective-permute-start(f32[3,4,2,4,128]{4,2,1,0,3:T(2,128)S(1)} %pad_maximum_fusion.3), channel_id=1, source_target_pairs={{1,0},{2,1},{3,2},{0,3},{5,4},{6,5},{7,6},{4,7},{9,8},{10,9},{11,1... | collective-permute-start | bytes 147464 | tf_op jit(solution)/shard_map/ppermute | solution.py:35
  15.6 0.0 collective-permute-start.3
  15.6 1.7 %collective-permute-done.4 = f32[3,4,2,4,128]{4,2,1,0,3:T(2,128)S(1)} collective-permute-done((f32[3,4,2,4,128]{4,2,1,0,3:T(2,128)S(1)}, f32[3,4,2,4,128]{4,2,1,0,3:T(2,128)S(1)}, u32[]{:S(2)}, u32[]{:S(2)}) %collective-permute-start.4) | collective-permute-done | bytes 49184 | tf_op jit(solution)/shard_map/ppermute | solution.py:35
  17.4 4.1 %collective-permute-done.3 = f32[3,4,2,4,128]{4,2,1,0,3:T(2,128)S(1)} collective-permute-done((f32[3,4,2,4,128]{4,2,1,0,3:T(2,128)S(1)}, f32[3,4,2,4,128]{4,2,1,0,3:T(2,128)S(1)}, u32[]{:S(2)}, u32[]{:S(2)}) %collective-permute-start.3) | collective-permute-done | bytes 49184 | tf_op jit(solution)/shard_map/ppermute | solution.py:34
  21.5 0.1 pad_maximum_fusion
  21.6 0.1 copy.7
  21.7 2.8 %density.3 = f32[8,128]{1,0:T(8,128)S(1)} custom-call(f32[72,8,128]{2,1,0:T(8,128)S(1)} %pad.10.feat_ref), custom_call_target="tpu_custom_call" | custom-call | tf_op jit(solution)/shard_map/density/pallas_call | solution.py:240
  24.6 0.1 collective-permute-start.5
  24.6 1.2 %collective-permute-done.5 = f32[1,2,4,128]{3,2,1,0:T(4,128)S(1)} collective-permute-done((f32[1,2,4,128]{3,2,1,0:T(4,128)S(1)}, f32[1,2,4,128]{3,2,1,0:T(4,128)S(1)}, u32[]{:S(2)}, u32[]{:S(2)}) %collective-permute-start.5) | collective-permute-done | bytes 4128 | tf_op jit(solution)/shard_map/ppermute | solution.py:25
  25.8 0.1 collective-permute-start.7
  25.9 2.0 %collective-permute-start.6 = (f32[1,4,4,128]{3,2,1,0:T(4,128)S(1)}, f32[1,4,4,128]{3,2,1,0:T(4,128)S(1)}, u32[]{:S(2)}, u32[]{:S(2)}) collective-permute-start(f32[1,4,4,128]{3,2,1,0:T(4,128)S(1)} %pad_maximum_fusion.13), channel_id=1, source_target_pairs={{0,8},{8,16},{16,24},{24,0},{1,9},{9,17},{17,25},{25,1},{2,10},{10... | collective-permute-start | bytes 24584 | tf_op jit(solution)/shard_map/ppermute | solution.py:34
  27.9 1.6 %collective-permute-done.7 = f32[1,4,4,128]{3,2,1,0:T(4,128)S(1)} collective-permute-done((f32[1,4,4,128]{3,2,1,0:T(4,128)S(1)}, f32[1,4,4,128]{3,2,1,0:T(4,128)S(1)}, u32[]{:S(2)}, u32[]{:S(2)}) %collective-permute-start.7) | collective-permute-done | bytes 8224 | tf_op jit(solution)/shard_map/ppermute | solution.py:35
  29.5 1.0 %collective-permute-done.6 = f32[1,4,4,128]{3,2,1,0:T(4,128)S(1)} collective-permute-done((f32[1,4,4,128]{3,2,1,0:T(4,128)S(1)}, f32[1,4,4,128]{3,2,1,0:T(4,128)S(1)}, u32[]{:S(2)}, u32[]{:S(2)}) %collective-permute-start.6) | collective-permute-done | bytes 8224 | tf_op jit(solution)/shard_map/ppermute | solution.py:34
  30.5 0.0 copy-start
  30.5 0.7 copy-done
  31.1 3.9 %force_first.1 = (f32[3,4,128]{2,1,0:T(4,128)S(1)}, f32[4,4,128]{2,1,0:T(4,128)S(1)}) custom-call(f32[72,8,128]{2,1,0:T(8,128)S(1)} %pad.10.feat_ref, f32[48,128]{1,0:T(8,128)S(1)} %bitcast.25, f32[3,4,128]{2,1,0:T(4,128)S(1)} %bitcast.44), custom_call_target="tpu_custom_call" | custom-call | tf_op jit(solution)/shard_map/force_first/pallas_call | solution.py:257
  35.0 0.1 collective-permute-start.8
  35.1 1.2 %collective-permute-done.8 = f32[1,2,2,4,128]{4,3,2,1,0:T(4,128)S(1)} collective-permute-done((f32[1,2,2,4,128]{4,3,2,1,0:T(4,128)S(1)}, f32[1,2,2,4,128]{4,3,2,1,0:T(4,128)S(1)}, u32[]{:S(2)}, u32[]{:S(2)}) %collective-permute-start.8) | collective-permute-done | bytes 8224 | tf_op jit(solution)/shard_map/ppermute | solution.py:25
  36.3 1.1 %collective-permute-start.10 = (f32[1,4,2,4,128]{4,3,2,1,0:T(4,128)S(1)}, f32[1,4,2,4,128]{4,3,2,1,0:T(4,128)S(1)}, u32[]{:S(2)}, u32[]{:S(2)}) collective-permute-start(f32[1,4,2,4,128]{4,3,2,1,0:T(4,128)S(1)} %pad_maximum_fusion.10), channel_id=1, source_target_pairs={{8,0},{16,8},{24,16},{0,24},{9,1},{17,9},{25,17},{1,25},{10,2},{18... | collective-permute-start | bytes 49160 | tf_op jit(solution)/shard_map/ppermute | solution.py:35
  37.3 1.0 %collective-permute-start.9 = (f32[1,4,2,4,128]{4,3,2,1,0:T(4,128)S(1)}, f32[1,4,2,4,128]{4,3,2,1,0:T(4,128)S(1)}, u32[]{:S(2)}, u32[]{:S(2)}) collective-permute-start(f32[1,4,2,4,128]{4,3,2,1,0:T(4,128)S(1)} %pad_maximum_fusion.10), channel_id=1, source_target_pairs={{0,8},{8,16},{16,24},{24,0},{1,9},{9,17},{17,25},{25,1},{2,10},{10... | collective-permute-start | bytes 49160 | tf_op jit(solution)/shard_map/ppermute | solution.py:34
  38.4 1.7 %collective-permute-done.10 = f32[1,4,2,4,128]{4,3,2,1,0:T(4,128)S(1)} collective-permute-done((f32[1,4,2,4,128]{4,3,2,1,0:T(4,128)S(1)}, f32[1,4,2,4,128]{4,3,2,1,0:T(4,128)S(1)}, u32[]{:S(2)}, u32[]{:S(2)}) %collective-permute-start.10) | collective-permute-done | bytes 16416 | tf_op jit(solution)/shard_map/ppermute | solution.py:35
  40.1 1.9 %collective-permute-done.9 = f32[1,4,2,4,128]{4,3,2,1,0:T(4,128)S(1)} collective-permute-done((f32[1,4,2,4,128]{4,3,2,1,0:T(4,128)S(1)}, f32[1,4,2,4,128]{4,3,2,1,0:T(4,128)S(1)}, u32[]{:S(2)}, u32[]{:S(2)}) %collective-permute-start.9) | collective-permute-done | bytes 16416 | tf_op jit(solution)/shard_map/ppermute | solution.py:34
  42.0 0.1 collective-permute-start.12
  42.1 2.0 %collective-permute-start.11 = (f32[3,4,2,4,128]{4,3,2,1,0:T(4,128)S(1)}, f32[3,4,2,4,128]{4,3,2,1,0:T(4,128)S(1)}, u32[]{:S(2)}, u32[]{:S(2)}) collective-permute-start(f32[3,4,2,4,128]{4,3,2,1,0:T(4,128)S(1)} %pad_maximum_fusion.4), channel_id=1, source_target_pairs={{0,1},{1,2},{2,3},{3,0},{4,5},{5,6},{6,7},{7,4},{8,9},{9,10},{10,1... | collective-permute-start | bytes 147464 | tf_op jit(solution)/shard_map/ppermute | solution.py:34
  44.1 2.2 %collective-permute-done.12 = f32[3,4,2,4,128]{4,3,2,1,0:T(4,128)S(1)} collective-permute-done((f32[3,4,2,4,128]{4,3,2,1,0:T(4,128)S(1)}, f32[3,4,2,4,128]{4,3,2,1,0:T(4,128)S(1)}, u32[]{:S(2)}, u32[]{:S(2)}) %collective-permute-start.12) | collective-permute-done | bytes 49184 | tf_op jit(solution)/shard_map/ppermute | solution.py:35
  46.3 1.7 %collective-permute-done.11 = f32[3,4,2,4,128]{4,3,2,1,0:T(4,128)S(1)} collective-permute-done((f32[3,4,2,4,128]{4,3,2,1,0:T(4,128)S(1)}, f32[3,4,2,4,128]{4,3,2,1,0:T(4,128)S(1)}, u32[]{:S(2)}, u32[]{:S(2)}) %collective-permute-start.11) | collective-permute-done | bytes 49184 | tf_op jit(solution)/shard_map/ppermute | solution.py:34
  48.1 2.8 %density.4 = f32[8,128]{1,0:T(8,128)S(1)} custom-call(f32[72,8,128]{2,1,0:T(8,128)S(1)} %pad.11.feat_ref), custom_call_target="tpu_custom_call" | custom-call | tf_op jit(solution)/shard_map/density/pallas_call | solution.py:240
  50.9 0.1 collective-permute-start.13
  51.0 1.2 %collective-permute-done.13 = f32[1,2,4,128]{3,2,1,0:T(4,128)S(1)} collective-permute-done((f32[1,2,4,128]{3,2,1,0:T(4,128)S(1)}, f32[1,2,4,128]{3,2,1,0:T(4,128)S(1)}, u32[]{:S(2)}, u32[]{:S(2)}) %collective-permute-start.13) | collective-permute-done | bytes 4128 | tf_op jit(solution)/shard_map/ppermute | solution.py:25
  52.2 0.3 collective-permute-start.15
  52.4 1.8 %collective-permute-start.14 = (f32[1,4,4,128]{3,2,1,0:T(4,128)S(1)}, f32[1,4,4,128]{3,2,1,0:T(4,128)S(1)}, u32[]{:S(2)}, u32[]{:S(2)}) collective-permute-start(f32[1,4,4,128]{3,2,1,0:T(4,128)S(1)} %pad_maximum_fusion.14), channel_id=1, source_target_pairs={{0,8},{8,16},{16,24},{24,0},{1,9},{9,17},{17,25},{25,1},{2,10},{10... | collective-permute-start | bytes 24584 | tf_op jit(solution)/shard_map/ppermute | solution.py:34
  54.2 1.6 %collective-permute-done.15 = f32[1,4,4,128]{3,2,1,0:T(4,128)S(1)} collective-permute-done((f32[1,4,4,128]{3,2,1,0:T(4,128)S(1)}, f32[1,4,4,128]{3,2,1,0:T(4,128)S(1)}, u32[]{:S(2)}, u32[]{:S(2)}) %collective-permute-start.15) | collective-permute-done | bytes 8224 | tf_op jit(solution)/shard_map/ppermute | solution.py:35
  55.9 1.1 %collective-permute-done.14 = f32[1,4,4,128]{3,2,1,0:T(4,128)S(1)} collective-permute-done((f32[1,4,4,128]{3,2,1,0:T(4,128)S(1)}, f32[1,4,4,128]{3,2,1,0:T(4,128)S(1)}, u32[]{:S(2)}, u32[]{:S(2)}) %collective-permute-start.14) | collective-permute-done | bytes 8224 | tf_op jit(solution)/shard_map/ppermute | solution.py:34
  57.0 4.5 %force_middle.1 = (f32[3,4,128]{2,1,0:T(4,128)S(1)}, f32[4,4,128]{2,1,0:T(4,128)S(1)}, f32[3,4,128]{2,1,0:T(4,128)}) custom-call(f32[72,8,128]{2,1,0:T(8,128)S(1)} %pad.11.feat_ref, f32[48,128]{1,0:T(8,128)S(1)} %bitcast.24, f32[3,4,128]{2,1,0:T(4,128)S(1)} %get-tuple-element.8.vel_ref), custom_call_target="tpu_custom_call" | custom-call | tf_op jit(solution)/shard_map/force_middle/pallas_call | solution.py:257
  61.5 0.0 collective-permute-start.16
  61.5 1.2 %collective-permute-done.16 = f32[1,2,2,4,128]{4,3,2,1,0:T(4,128)S(1)} collective-permute-done((f32[1,2,2,4,128]{4,3,2,1,0:T(4,128)S(1)}, f32[1,2,2,4,128]{4,3,2,1,0:T(4,128)S(1)}, u32[]{:S(2)}, u32[]{:S(2)}) %collective-permute-start.16) | collective-permute-done | bytes 8224 | tf_op jit(solution)/shard_map/ppermute | solution.py:25
  62.7 1.9 %collective-permute-start.18 = (f32[1,4,2,4,128]{4,3,2,1,0:T(4,128)S(1)}, f32[1,4,2,4,128]{4,3,2,1,0:T(4,128)S(1)}, u32[]{:S(2)}, u32[]{:S(2)}) collective-permute-start(f32[1,4,2,4,128]{4,3,2,1,0:T(4,128)S(1)} %pad_maximum_fusion.11), channel_id=1, source_target_pairs={{8,0},{16,8},{24,16},{0,24},{9,1},{17,9},{25,17},{1,25},{10,2},{18... | collective-permute-start | bytes 49160 | tf_op jit(solution)/shard_map/ppermute | solution.py:35
  64.5 0.2 collective-permute-start.17
  64.7 1.7 %collective-permute-done.18 = f32[1,4,2,4,128]{4,3,2,1,0:T(4,128)S(1)} collective-permute-done((f32[1,4,2,4,128]{4,3,2,1,0:T(4,128)S(1)}, f32[1,4,2,4,128]{4,3,2,1,0:T(4,128)S(1)}, u32[]{:S(2)}, u32[]{:S(2)}) %collective-permute-start.18) | collective-permute-done | bytes 16416 | tf_op jit(solution)/shard_map/ppermute | solution.py:35
  66.5 2.7 %collective-permute-done.17 = f32[1,4,2,4,128]{4,3,2,1,0:T(4,128)S(1)} collective-permute-done((f32[1,4,2,4,128]{4,3,2,1,0:T(4,128)S(1)}, f32[1,4,2,4,128]{4,3,2,1,0:T(4,128)S(1)}, u32[]{:S(2)}, u32[]{:S(2)}) %collective-permute-start.17) | collective-permute-done | bytes 16416 | tf_op jit(solution)/shard_map/ppermute | solution.py:34
  69.2 0.1 collective-permute-start.20
  69.3 2.0 %collective-permute-start.19 = (f32[3,4,2,4,128]{4,3,2,1,0:T(4,128)S(1)}, f32[3,4,2,4,128]{4,3,2,1,0:T(4,128)S(1)}, u32[]{:S(2)}, u32[]{:S(2)}) collective-permute-start(f32[3,4,2,4,128]{4,3,2,1,0:T(4,128)S(1)} %pad_maximum_fusion.5), channel_id=1, source_target_pairs={{0,1},{1,2},{2,3},{3,0},{4,5},{5,6},{6,7},{7,4},{8,9},{9,10},{10,1... | collective-permute-start | bytes 147464 | tf_op jit(solution)/shard_map/ppermute | solution.py:34
  71.3 2.3 %collective-permute-done.20 = f32[3,4,2,4,128]{4,3,2,1,0:T(4,128)S(1)} collective-permute-done((f32[3,4,2,4,128]{4,3,2,1,0:T(4,128)S(1)}, f32[3,4,2,4,128]{4,3,2,1,0:T(4,128)S(1)}, u32[]{:S(2)}, u32[]{:S(2)}) %collective-permute-start.20) | collective-permute-done | bytes 49184 | tf_op jit(solution)/shard_map/ppermute | solution.py:35
  73.6 1.6 %collective-permute-done.19 = f32[3,4,2,4,128]{4,3,2,1,0:T(4,128)S(1)} collective-permute-done((f32[3,4,2,4,128]{4,3,2,1,0:T(4,128)S(1)}, f32[3,4,2,4,128]{4,3,2,1,0:T(4,128)S(1)}, u32[]{:S(2)}, u32[]{:S(2)}) %collective-permute-start.19) | collective-permute-done | bytes 49184 | tf_op jit(solution)/shard_map/ppermute | solution.py:34
  75.3 2.8 %density.5 = f32[8,128]{1,0:T(8,128)S(1)} custom-call(f32[72,8,128]{2,1,0:T(8,128)S(1)} %pad.12.feat_ref), custom_call_target="tpu_custom_call" | custom-call | tf_op jit(solution)/shard_map/density/pallas_call | solution.py:240
  78.1 0.1 collective-permute-start.21
  78.2 1.2 %collective-permute-done.21 = f32[1,2,4,128]{3,2,1,0:T(4,128)S(1)} collective-permute-done((f32[1,2,4,128]{3,2,1,0:T(4,128)S(1)}, f32[1,2,4,128]{3,2,1,0:T(4,128)S(1)}, u32[]{:S(2)}, u32[]{:S(2)}) %collective-permute-start.21) | collective-permute-done | bytes 4128 | tf_op jit(solution)/shard_map/ppermute | solution.py:25
  79.3 0.3 collective-permute-start.23
  79.6 1.8 %collective-permute-start.22 = (f32[1,4,4,128]{3,2,1,0:T(4,128)S(1)}, f32[1,4,4,128]{3,2,1,0:T(4,128)S(1)}, u32[]{:S(2)}, u32[]{:S(2)}) collective-permute-start(f32[1,4,4,128]{3,2,1,0:T(4,128)S(1)} %pad_maximum_fusion.15), channel_id=1, source_target_pairs={{0,8},{8,16},{16,24},{24,0},{1,9},{9,17},{17,25},{25,1},{2,10},{10... | collective-permute-start | bytes 24584 | tf_op jit(solution)/shard_map/ppermute | solution.py:34
  81.4 1.6 %collective-permute-done.23 = f32[1,4,4,128]{3,2,1,0:T(4,128)S(1)} collective-permute-done((f32[1,4,4,128]{3,2,1,0:T(4,128)S(1)}, f32[1,4,4,128]{3,2,1,0:T(4,128)S(1)}, u32[]{:S(2)}, u32[]{:S(2)}) %collective-permute-start.23) | collective-permute-done | bytes 8224 | tf_op jit(solution)/shard_map/ppermute | solution.py:35
  83.0 1.2 %collective-permute-done.22 = f32[1,4,4,128]{3,2,1,0:T(4,128)S(1)} collective-permute-done((f32[1,4,4,128]{3,2,1,0:T(4,128)S(1)}, f32[1,4,4,128]{3,2,1,0:T(4,128)S(1)}, u32[]{:S(2)}, u32[]{:S(2)}) %collective-permute-start.22) | collective-permute-done | bytes 8224 | tf_op jit(solution)/shard_map/ppermute | solution.py:34
  84.2 4.5 %force_last.1 = f32[3,4,128]{2,1,0:T(4,128)} custom-call(f32[72,8,128]{2,1,0:T(8,128)S(1)} %pad.12.feat_ref, f32[48,128]{1,0:T(8,128)S(1)} %bitcast.26, f32[3,4,128]{2,1,0:T(4,128)S(1)} %get-tuple-element.11.vel_ref), custom_call_target="tpu_custom_call" | custom-call | tf_op jit(solution)/shard_map/force_last/pallas_call | solution.py:257
  (24 shorter events, 0.3 us)
Async XLA Ops:
  0.6 0.7 copy-start.2
  0.6 1.4 %copy-start.1 = (f32[3,1,2,2,128]{4,3,2,1,0:T(2,128)S(1)}, f32[3,1,2,2,128]{4,3,2,1,0:T(2,128)}, u32[]{:S(2)}) copy-start(f32[3,1,2,2,128]{4,3,2,1,0:T(2,128)} %param.4) | copy-start | bytes 18436
  2.1 1.4 %collective-permute-start = (f32[1,2,2,4,128]{4,2,1,0,3:T(2,128)S(1)}, f32[1,2,2,4,128]{4,2,1,0,3:T(2,128)S(1)}, u32[]{:S(2)}, u32[]{:S(2)}) collective-permute-start(f32[1,2,2,4,128]{4,2,1,0,3:T(2,128)S(1)} %pad_maximum_fusion.12), channel_id=1, source_target_pairs={{0,4},{4,0},{1,5},{5,1},{2,6},{6,2},{3,7},{7,3},{8,12},{12,8},{9,1... | collective-permute-start | bytes 24584 | tf_op jit(solution)/shard_map/ppermute | solution.py:25
  3.5 5.3 %collective-permute-start.2 = (f32[1,4,2,4,128]{4,2,1,0,3:T(2,128)S(1)}, f32[1,4,2,4,128]{4,2,1,0,3:T(2,128)S(1)}, u32[]{:S(2)}, u32[]{:S(2)}) collective-permute-start(f32[1,4,2,4,128]{4,2,1,0,3:T(2,128)S(1)} %pad_maximum_fusion.9), channel_id=1, source_target_pairs={{8,0},{16,8},{24,16},{0,24},{9,1},{17,9},{25,17},{1,25},{10,2},{18... | collective-permute-start | bytes 49160 | tf_op jit(solution)/shard_map/ppermute | solution.py:35
  7.3 4.6 %collective-permute-start.1 = (f32[1,4,2,4,128]{4,2,1,0,3:T(2,128)S(1)}, f32[1,4,2,4,128]{4,2,1,0,3:T(2,128)S(1)}, u32[]{:S(2)}, u32[]{:S(2)}) collective-permute-start(f32[1,4,2,4,128]{4,2,1,0,3:T(2,128)S(1)} %pad_maximum_fusion.9), channel_id=1, source_target_pairs={{0,8},{8,16},{16,24},{24,0},{1,9},{9,17},{17,25},{25,1},{2,10},{10... | collective-permute-start | bytes 49160 | tf_op jit(solution)/shard_map/ppermute | solution.py:34
  12.0 5.4 %collective-permute-start.4 = (f32[3,4,2,4,128]{4,2,1,0,3:T(2,128)S(1)}, f32[3,4,2,4,128]{4,2,1,0,3:T(2,128)S(1)}, u32[]{:S(2)}, u32[]{:S(2)}) collective-permute-start(f32[3,4,2,4,128]{4,2,1,0,3:T(2,128)S(1)} %pad_maximum_fusion.3), channel_id=1, source_target_pairs={{1,0},{2,1},{3,2},{0,3},{5,4},{6,5},{7,6},{4,7},{9,8},{10,9},{11,1... | collective-permute-start | bytes 147464 | tf_op jit(solution)/shard_map/ppermute | solution.py:35
  15.6 5.9 %collective-permute-start.3 = (f32[3,4,2,4,128]{4,2,1,0,3:T(2,128)S(1)}, f32[3,4,2,4,128]{4,2,1,0,3:T(2,128)S(1)}, u32[]{:S(2)}, u32[]{:S(2)}) collective-permute-start(f32[3,4,2,4,128]{4,2,1,0,3:T(2,128)S(1)} %pad_maximum_fusion.3), channel_id=1, source_target_pairs={{0,1},{1,2},{2,3},{3,0},{4,5},{5,6},{6,7},{7,4},{8,9},{9,10},{10,1... | collective-permute-start | bytes 147464 | tf_op jit(solution)/shard_map/ppermute | solution.py:34
  24.6 1.2 %collective-permute-start.5 = (f32[1,2,4,128]{3,2,1,0:T(4,128)S(1)}, f32[1,2,4,128]{3,2,1,0:T(4,128)S(1)}, u32[]{:S(2)}, u32[]{:S(2)}) collective-permute-start(f32[1,2,4,128]{3,2,1,0:T(4,128)S(1)} %bitcast.35), channel_id=1, source_target_pairs={{0,4},{4,0},{1,5},{5,1},{2,6},{6,2},{3,7},{7,3},{8,12},{12,8},{9,1... | collective-permute-start | bytes 12296 | tf_op jit(solution)/shard_map/ppermute | solution.py:25
  25.8 3.7 %collective-permute-start.7 = (f32[1,4,4,128]{3,2,1,0:T(4,128)S(1)}, f32[1,4,4,128]{3,2,1,0:T(4,128)S(1)}, u32[]{:S(2)}, u32[]{:S(2)}) collective-permute-start(f32[1,4,4,128]{3,2,1,0:T(4,128)S(1)} %pad_maximum_fusion.13), channel_id=1, source_target_pairs={{8,0},{16,8},{24,16},{0,24},{9,1},{17,9},{25,17},{1,25},{10,2},{18... | collective-permute-start | bytes 24584 | tf_op jit(solution)/shard_map/ppermute | solution.py:35
  25.9 4.6 %collective-permute-start.6 = (f32[1,4,4,128]{3,2,1,0:T(4,128)S(1)}, f32[1,4,4,128]{3,2,1,0:T(4,128)S(1)}, u32[]{:S(2)}, u32[]{:S(2)}) collective-permute-start(f32[1,4,4,128]{3,2,1,0:T(4,128)S(1)} %pad_maximum_fusion.13), channel_id=1, source_target_pairs={{0,8},{8,16},{16,24},{24,0},{1,9},{9,17},{17,25},{25,1},{2,10},{10... | collective-permute-start | bytes 24584 | tf_op jit(solution)/shard_map/ppermute | solution.py:34
  30.5 0.7 copy-start
  35.0 1.2 %collective-permute-start.8 = (f32[1,2,2,4,128]{4,3,2,1,0:T(4,128)S(1)}, f32[1,2,2,4,128]{4,3,2,1,0:T(4,128)S(1)}, u32[]{:S(2)}, u32[]{:S(2)}) collective-permute-start(f32[1,2,2,4,128]{4,3,2,1,0:T(4,128)S(1)} %bitcast.31), channel_id=1, source_target_pairs={{0,4},{4,0},{1,5},{5,1},{2,6},{6,2},{3,7},{7,3},{8,12},{12,8},{9,1... | collective-permute-start | bytes 24584 | tf_op jit(solution)/shard_map/ppermute | solution.py:25
  36.3 3.8 %collective-permute-start.10 = (f32[1,4,2,4,128]{4,3,2,1,0:T(4,128)S(1)}, f32[1,4,2,4,128]{4,3,2,1,0:T(4,128)S(1)}, u32[]{:S(2)}, u32[]{:S(2)}) collective-permute-start(f32[1,4,2,4,128]{4,3,2,1,0:T(4,128)S(1)} %pad_maximum_fusion.10), channel_id=1, source_target_pairs={{8,0},{16,8},{24,16},{0,24},{9,1},{17,9},{25,17},{1,25},{10,2},{18... | collective-permute-start | bytes 49160 | tf_op jit(solution)/shard_map/ppermute | solution.py:35
  37.3 4.6 %collective-permute-start.9 = (f32[1,4,2,4,128]{4,3,2,1,0:T(4,128)S(1)}, f32[1,4,2,4,128]{4,3,2,1,0:T(4,128)S(1)}, u32[]{:S(2)}, u32[]{:S(2)}) collective-permute-start(f32[1,4,2,4,128]{4,3,2,1,0:T(4,128)S(1)} %pad_maximum_fusion.10), channel_id=1, source_target_pairs={{0,8},{8,16},{16,24},{24,0},{1,9},{9,17},{17,25},{25,1},{2,10},{10... | collective-permute-start | bytes 49160 | tf_op jit(solution)/shard_map/ppermute | solution.py:34
  42.0 4.3 %collective-permute-start.12 = (f32[3,4,2,4,128]{4,3,2,1,0:T(4,128)S(1)}, f32[3,4,2,4,128]{4,3,2,1,0:T(4,128)S(1)}, u32[]{:S(2)}, u32[]{:S(2)}) collective-permute-start(f32[3,4,2,4,128]{4,3,2,1,0:T(4,128)S(1)} %pad_maximum_fusion.4), channel_id=1, source_target_pairs={{1,0},{2,1},{3,2},{0,3},{5,4},{6,5},{7,6},{4,7},{9,8},{10,9},{11,1... | collective-permute-start | bytes 147464 | tf_op jit(solution)/shard_map/ppermute | solution.py:35
  42.1 5.9 %collective-permute-start.11 = (f32[3,4,2,4,128]{4,3,2,1,0:T(4,128)S(1)}, f32[3,4,2,4,128]{4,3,2,1,0:T(4,128)S(1)}, u32[]{:S(2)}, u32[]{:S(2)}) collective-permute-start(f32[3,4,2,4,128]{4,3,2,1,0:T(4,128)S(1)} %pad_maximum_fusion.4), channel_id=1, source_target_pairs={{0,1},{1,2},{2,3},{3,0},{4,5},{5,6},{6,7},{7,4},{8,9},{9,10},{10,1... | collective-permute-start | bytes 147464 | tf_op jit(solution)/shard_map/ppermute | solution.py:34
  50.9 1.2 %collective-permute-start.13 = (f32[1,2,4,128]{3,2,1,0:T(4,128)S(1)}, f32[1,2,4,128]{3,2,1,0:T(4,128)S(1)}, u32[]{:S(2)}, u32[]{:S(2)}) collective-permute-start(f32[1,2,4,128]{3,2,1,0:T(4,128)S(1)} %bitcast.38), channel_id=1, source_target_pairs={{0,4},{4,0},{1,5},{5,1},{2,6},{6,2},{3,7},{7,3},{8,12},{12,8},{9,1... | collective-permute-start | bytes 12296 | tf_op jit(solution)/shard_map/ppermute | solution.py:25
  52.2 3.7 %collective-permute-start.15 = (f32[1,4,4,128]{3,2,1,0:T(4,128)S(1)}, f32[1,4,4,128]{3,2,1,0:T(4,128)S(1)}, u32[]{:S(2)}, u32[]{:S(2)}) collective-permute-start(f32[1,4,4,128]{3,2,1,0:T(4,128)S(1)} %pad_maximum_fusion.14), channel_id=1, source_target_pairs={{8,0},{16,8},{24,16},{0,24},{9,1},{17,9},{25,17},{1,25},{10,2},{18... | collective-permute-start | bytes 24584 | tf_op jit(solution)/shard_map/ppermute | solution.py:35
  52.4 4.6 %collective-permute-start.14 = (f32[1,4,4,128]{3,2,1,0:T(4,128)S(1)}, f32[1,4,4,128]{3,2,1,0:T(4,128)S(1)}, u32[]{:S(2)}, u32[]{:S(2)}) collective-permute-start(f32[1,4,4,128]{3,2,1,0:T(4,128)S(1)} %pad_maximum_fusion.14), channel_id=1, source_target_pairs={{0,8},{8,16},{16,24},{24,0},{1,9},{9,17},{17,25},{25,1},{2,10},{10... | collective-permute-start | bytes 24584 | tf_op jit(solution)/shard_map/ppermute | solution.py:34
  61.5 1.2 %collective-permute-start.16 = (f32[1,2,2,4,128]{4,3,2,1,0:T(4,128)S(1)}, f32[1,2,2,4,128]{4,3,2,1,0:T(4,128)S(1)}, u32[]{:S(2)}, u32[]{:S(2)}) collective-permute-start(f32[1,2,2,4,128]{4,3,2,1,0:T(4,128)S(1)} %bitcast.27), channel_id=1, source_target_pairs={{0,4},{4,0},{1,5},{5,1},{2,6},{6,2},{3,7},{7,3},{8,12},{12,8},{9,1... | collective-permute-start | bytes 24584 | tf_op jit(solution)/shard_map/ppermute | solution.py:25
  62.7 3.8 %collective-permute-start.18 = (f32[1,4,2,4,128]{4,3,2,1,0:T(4,128)S(1)}, f32[1,4,2,4,128]{4,3,2,1,0:T(4,128)S(1)}, u32[]{:S(2)}, u32[]{:S(2)}) collective-permute-start(f32[1,4,2,4,128]{4,3,2,1,0:T(4,128)S(1)} %pad_maximum_fusion.11), channel_id=1, source_target_pairs={{8,0},{16,8},{24,16},{0,24},{9,1},{17,9},{25,17},{1,25},{10,2},{18... | collective-permute-start | bytes 49160 | tf_op jit(solution)/shard_map/ppermute | solution.py:35
  64.5 4.6 %collective-permute-start.17 = (f32[1,4,2,4,128]{4,3,2,1,0:T(4,128)S(1)}, f32[1,4,2,4,128]{4,3,2,1,0:T(4,128)S(1)}, u32[]{:S(2)}, u32[]{:S(2)}) collective-permute-start(f32[1,4,2,4,128]{4,3,2,1,0:T(4,128)S(1)} %pad_maximum_fusion.11), channel_id=1, source_target_pairs={{0,8},{8,16},{16,24},{24,0},{1,9},{9,17},{17,25},{25,1},{2,10},{10... | collective-permute-start | bytes 49160 | tf_op jit(solution)/shard_map/ppermute | solution.py:34
  69.2 4.4 %collective-permute-start.20 = (f32[3,4,2,4,128]{4,3,2,1,0:T(4,128)S(1)}, f32[3,4,2,4,128]{4,3,2,1,0:T(4,128)S(1)}, u32[]{:S(2)}, u32[]{:S(2)}) collective-permute-start(f32[3,4,2,4,128]{4,3,2,1,0:T(4,128)S(1)} %pad_maximum_fusion.5), channel_id=1, source_target_pairs={{1,0},{2,1},{3,2},{0,3},{5,4},{6,5},{7,6},{4,7},{9,8},{10,9},{11,1... | collective-permute-start | bytes 147464 | tf_op jit(solution)/shard_map/ppermute | solution.py:35
  69.3 5.9 %collective-permute-start.19 = (f32[3,4,2,4,128]{4,3,2,1,0:T(4,128)S(1)}, f32[3,4,2,4,128]{4,3,2,1,0:T(4,128)S(1)}, u32[]{:S(2)}, u32[]{:S(2)}) collective-permute-start(f32[3,4,2,4,128]{4,3,2,1,0:T(4,128)S(1)} %pad_maximum_fusion.5), channel_id=1, source_target_pairs={{0,1},{1,2},{2,3},{3,0},{4,5},{5,6},{6,7},{7,4},{8,9},{9,10},{10,1... | collective-permute-start | bytes 147464 | tf_op jit(solution)/shard_map/ppermute | solution.py:34
  78.1 1.2 %collective-permute-start.21 = (f32[1,2,4,128]{3,2,1,0:T(4,128)S(1)}, f32[1,2,4,128]{3,2,1,0:T(4,128)S(1)}, u32[]{:S(2)}, u32[]{:S(2)}) collective-permute-start(f32[1,2,4,128]{3,2,1,0:T(4,128)S(1)} %bitcast.41), channel_id=1, source_target_pairs={{0,4},{4,0},{1,5},{5,1},{2,6},{6,2},{3,7},{7,3},{8,12},{12,8},{9,1... | collective-permute-start | bytes 12296 | tf_op jit(solution)/shard_map/ppermute | solution.py:25
  79.3 3.7 %collective-permute-start.23 = (f32[1,4,4,128]{3,2,1,0:T(4,128)S(1)}, f32[1,4,4,128]{3,2,1,0:T(4,128)S(1)}, u32[]{:S(2)}, u32[]{:S(2)}) collective-permute-start(f32[1,4,4,128]{3,2,1,0:T(4,128)S(1)} %pad_maximum_fusion.15), channel_id=1, source_target_pairs={{8,0},{16,8},{24,16},{0,24},{9,1},{17,9},{25,17},{1,25},{10,2},{18... | collective-permute-start | bytes 24584 | tf_op jit(solution)/shard_map/ppermute | solution.py:35
  79.6 4.5 %collective-permute-start.22 = (f32[1,4,4,128]{3,2,1,0:T(4,128)S(1)}, f32[1,4,4,128]{3,2,1,0:T(4,128)S(1)}, u32[]{:S(2)}, u32[]{:S(2)}) collective-permute-start(f32[1,4,4,128]{3,2,1,0:T(4,128)S(1)} %pad_maximum_fusion.15), channel_id=1, source_target_pairs={{0,8},{8,16},{16,24},{24,0},{1,9},{9,17},{17,25},{25,1},{2,10},{10... | collective-permute-start | bytes 24584 | tf_op jit(solution)/shard_map/ppermute | solution.py:34
